TPU v7x, 256 devices: a whole 4x4x8 slice. The times are simulated.
256 devices in a mesh: sym: 4 (over z_hi, core), dev: 64 (over y, z_lo, x).
Axes of the slice: x: 4, y: 4, z: 8 (z_hi: 2, z_lo: 4; z = z_hi * 4 + z_lo), core: 2. Of those that a mesh axis runs over, the one named last changes fastest.
Arguments:
- inner_state: float32 [8, 2, 4096], P('sym', None, 'dev'), may hold values from -6 to 6
- block_sizes: int32 [8], replicated, may hold values from 1024 to 4096, as said below
- block_ham: bfloat16 [8, 4096, 4096], P('sym', 'dev'), as said below
- dipole_inner: bfloat16 [8, 4096, 4096], P('sym', 'dev'), may hold values from -0.09375 to 0.09375
- surface_amps: bfloat16 [800, 4096], P(None, 'dev'), may hold values from -0.29882812 to 0.29882812
- channel_block: int32 [800, 1], replicated, may hold values from 0 to 7
- outer_state: float32 [2, 800, 32768], P(None, None, ('sym', 'dev')), may hold values from -6 to 6
- channel_energy: float32 [800], replicated, may hold values from 2 to 40
- laser_dipole: bfloat16 [800, 800], replicated, as said below
Outputs:
- inner_next: float32 [8, 2, 4096], P('sym', None, 'dev')
- outer_next: float32 [2, 800, 32768], P(None, None, ('sym', 'dev'))
Inputs may be any that keep to these rules, and one draw needn't show every extreme that they name: `block_sizes`: live states of each block; some block has exactly 4096. `channel_block`: every block has at least one channel. `block_ham`: each block is a symmetric matrix. `laser_dipole`: Symmetric.
All inputs are finite; a program needn't handle non-finite values.
Results may differ from a plain program's by a relative error of at most 0.0035.
Values may be sent and summed in bfloat16 or wider, within the bound.
A program may use at most 64 MiB of HBM per device.

v0:
```python
import jax
import jax.numpy as jnp
from jax import lax
from jax.sharding import PartitionSpec as P

TERMS = 4


time_step = 0.012
spacing = 0.1
kinetic = 0.5 / (spacing * spacing)
block_scale = 90.0
dipole_scale = 40.0
laser_scale = 25.0


def padded(block, sides, width):
    for axis, dim in sides:
        count = lax.axis_size(axis)
        forward = [(i, i + 1) for i in range(count - 1)]
        backward = [(target, source) for source, target in forward]
        low = lax.ppermute(
            lax.slice_in_dim(block, block.shape[dim] - width, None, axis=dim), axis, forward
        )
        high = lax.ppermute(lax.slice_in_dim(block, 0, width, axis=dim), axis, backward)
        block = jnp.concatenate([low, block, high], axis=dim)
    return block


def shifted_2(block, axis, distance):
    devices = range(lax.axis_size(axis))
    route = [(i - distance, i) for i in devices if i - distance in devices]
    return lax.ppermute(block, axis, route)


def outer_local(values, boundary_sum, is_root, channel_energy, laser_dipole):
    edges = jnp.concatenate([values[:, :, :1], values[:, :, -1:]], axis=2)
    extended = padded(edges, ((("sym", "dev"), 2),), 1)
    left_cells = jnp.where(is_root, boundary_sum, extended[:, :, 0])
    right_cells = extended[:, :, 3]
    shifted = jnp.concatenate([left_cells[:, :, None], values[:, :, :-1]], axis=2)
    ahead = jnp.concatenate([values[:, :, 1:], right_cells[:, :, None]], axis=2)
    curvature = shifted - 2.0 * values + ahead
    mixed_term = jnp.einsum(
        "cd,idn->icn", laser_dipole, values.astype(jnp.bfloat16), preferred_element_type=jnp.float32
    )
    return -kinetic * curvature + channel_energy[None, :, None] * values + laser_scale * mixed_term


def on_device(
    inner_state,
    block_sizes,
    block_ham,
    dipole_inner,
    surface_amps,
    channel_block,
    outer_state,
    channel_energy,
    laser_dipole,
):
    members = lax.axis_size("dev")
    group_index = lax.axis_index("sym")
    member_index = lax.axis_index("dev")
    position = group_index * members + member_index
    is_root = position == 0
    per_group = inner_state.shape[0]
    row_count = inner_state.shape[2]
    first_block = group_index * per_group
    local_sizes = lax.dynamic_slice_in_dim(block_sizes, first_block, per_group)
    row_index = member_index * row_count + jnp.arange(row_count, dtype=jnp.int32)
    live_rows = (row_index[None, :] < local_sizes[:, None])[:, None, :]
    owners = channel_block[:, 0]
    block_ids = first_block + jnp.arange(per_group, dtype=jnp.int32)
    onehot = owners[None, :] == block_ids[:, None]
    onehot_wide = onehot.astype(jnp.float32)
    onehot_half = onehot.astype(jnp.bfloat16)
    inner_now = jnp.where(live_rows, inner_state, jnp.float32(0.0))
    inner_sum = inner_now
    outer_sum = outer_state
    inner_term = inner_now
    outer_term = outer_state
    for degree in range(1, TERMS + 1):
        factor = time_step / degree
        state_half = inner_term.astype(jnp.bfloat16)
        real_cells = outer_term[:, :, 0:3]
        slope_half = (
            (-3.0 * real_cells[:, :, 0] + 4.0 * real_cells[:, :, 1] - real_cells[:, :, 2])
            * (0.5 / spacing)
        ).astype(jnp.bfloat16)
        partial_values = jnp.einsum(
            "cr,jir->jic", surface_amps, state_half, preferred_element_type=jnp.float32
        )
        boundary_part = jnp.sum(partial_values * onehot_wide[:, None, :], axis=0)
        slope_part = jnp.where(is_root, slope_half.astype(jnp.float32), jnp.float32(0.0))
        boundary_sum, slope_sum = lax.psum((boundary_part, slope_part), ("sym", "dev"))
        slope_all = slope_sum.astype(jnp.bfloat16)
        masked = onehot_half[:, None, :] * slope_all[None]
        bloch_term = jnp.einsum(
            "jic,cr->jir", masked, surface_amps, preferred_element_type=jnp.float32
        )
        transposed = jnp.einsum(
            "jrk,jir->jik", dipole_inner, state_half, preferred_element_type=jnp.float32
        )
        own_blocks = lax.all_gather(state_half, "dev", axis=2, tiled=True)
        from_above = shifted_2(own_blocks[0], "sym", -1)
        upper_blocks = jnp.concatenate([own_blocks[1:], from_above[None]], axis=0)
        diagonal_part = jnp.einsum(
            "jrk,jik->jir", block_ham, own_blocks, preferred_element_type=jnp.float32
        )
        forward = jnp.einsum(
            "jrk,jik->jir", dipole_inner, upper_blocks, preferred_element_type=jnp.float32
        )
        summed = lax.psum_scatter(transposed, "dev", scatter_dimension=2, tiled=True)
        from_below = shifted_2(summed[per_group - 1], "sym", 1)
        lower_part = jnp.concatenate([from_below[None], summed[:-1]], axis=0)
        diagonal_part, forward, lower_part = (diagonal_part, forward, lower_part)
        image = jnp.where(
            live_rows,
            block_scale * diagonal_part + dipole_scale * (forward + lower_part) + bloch_term,
            jnp.float32(0.0),
        )
        inner_term = factor * jnp.stack([image[:, 1], -image[:, 0]], axis=1)
        inner_sum = inner_sum + inner_term
        outer_image = outer_local(outer_term, boundary_sum, is_root, channel_energy, laser_dipole)
        outer_term = factor * jnp.stack([outer_image[1], -outer_image[0]])
        outer_sum = outer_sum + outer_term
    return (inner_sum, outer_sum)


def solution(mesh):
    placed = (
        P("sym", None, "dev"),
        P(),
        P("sym", "dev", None),
        P("sym", "dev", None),
        P(None, "dev"),
        P(),
        P(None, None, ("sym", "dev")),
        P(),
        P(),
    )
    return jax.shard_map(
        on_device,
        mesh=mesh,
        in_specs=placed,
        out_specs=(P("sym", None, "dev"), P(None, None, ("sym", "dev"))),
        check_vma=False,
    )
```

profile of v0, /device:TPU:1, one launch (start us, length us, event | category | flops | bytes accessed | tf_op | source)
XLA Modules:
  0.0 2080.3 jit_solution(10238117724803592112)
XLA Ops:
  9.5 182.2 %all_gather.12 = bf16[2,2,4096]{1,0,2:T(2,128)(2,1)} all-gather(bf16[2,2,64]{1,0,2:T(2,128)(2,1)S(1)} %copy.57), channel_id=1, replica_groups=mesh['sym'=4,'dev'=64] {'dev'}, dimensions={2}, use_global_device_ids=true | all-gather | bytes 33280 | tf_op jit(solution)/shard_map/all_gather | solution.py:104
  191.6 4.9 copy.58
  197.2 30.5 %collective-permute-start = (bf16[2,4096]{1,0:T(2,128)(2,1)}, bf16[2,4096]{1,0:T(2,128)(2,1)}, u32[]{:S(2)}, u32[]{:S(2)}) collective-permute-start(bf16[2,4096]{1,0:T(2,128)(2,1)} %get-tuple-element.53), channel_id=1, source_target_pairs={{64,0},{128,64},{192,128},{65,1},{129,65},{193,129},{66,2},{130,66... | collective-permute-start | bytes 49160 | tf_op jit(solution)/shard_map/ppermute | solution.py:33
  228.0 4.3 copy.89
  232.4 5.4 reshape.146
  245.5 9.6 collective-permute-start.5
  259.0 74.3 %all-reduce.3 = (f32[2,800]{1,0:T(2,128)S(1)}, bf16[2,800]{1,0:T(2,128)(2,1)S(1)}) all-reduce(f32[2,800]{1,0:T(2,128)S(1)} %fusion.44, f32[2,800]{1,0:T(2,128)S(1)} %get-tuple-element.37), channel_id=1, replica_groups=mesh['sym'=4,'dev'=64] {'sym','dev'}, use_global_device_ids=true, to_apply=%region_4.5 | all-reduce | flops 3200 | bytes 22400 | tf_op jit(solution)/shard_map/psum | solution.py:95
  345.3 7.1 collective-permute-start.9
  352.4 208.2 %reduce-scatter.13.cloned.1.call-done = f32[64,4]{1,0:T(8,128)} async-done(((f32[4096,4]{1,0:T(8,128)}), f32[64,4]{1,0:T(8,128)}) %reduce-scatter.13.cloned.1.call-update) | async-done | bytes 1040
  561.6 56.3 %collective-permute-start.1 = (f32[2,64]{1,0:T(2,128)S(1)}, f32[2,64]{1,0:T(2,128)S(1)}, u32[]{:S(2)}, u32[]{:S(2)}) collective-permute-start(f32[2,64]{1,0:T(2,128)S(1)} %bitcast.151), channel_id=1, source_target_pairs={{0,64},{64,128},{128,192},{1,65},{65,129},{129,193},{2,66},{66,130... | collective-permute-start | bytes 1544 | tf_op jit(solution)/shard_map/ppermute | solution.py:33
  628.6 74.8 %all-reduce.2 = (f32[2,800]{1,0:T(2,128)}, bf16[2,800]{1,0:T(2,128)(2,1)}) all-reduce(f32[2,800]{1,0:T(2,128)S(1)} %fusion.45, f32[2,800]{1,0:T(2,128)S(1)} %copy-done.18), channel_id=1, replica_groups=mesh['sym'=4,'dev'=64] {'sym','dev'}, use_global_device_ids=true, to_apply=%region_8.9 | all-reduce | flops 3200 | bytes 22400 | tf_op jit(solution)/shard_map/psum | solution.py:95
  713.3 4.3 copy.91
  717.6 5.4 reshape.148
  723.0 179.5 %all_gather.13 = bf16[2,2,4096]{1,0,2:T(2,128)(2,1)} all-gather(bf16[2,2,64]{1,0,2:T(2,128)(2,1)S(1)} %copy.61), channel_id=1, replica_groups=mesh['sym'=4,'dev'=64] {'dev'}, dimensions={2}, use_global_device_ids=true | all-gather | bytes 33280 | tf_op jit(solution)/shard_map/all_gather | solution.py:104
  902.5 4.8 copy.62
  908.0 26.3 %collective-permute-start.2 = (bf16[2,4096]{1,0:T(2,128)(2,1)}, bf16[2,4096]{1,0:T(2,128)(2,1)}, u32[]{:S(2)}, u32[]{:S(2)}) collective-permute-start(bf16[2,4096]{1,0:T(2,128)(2,1)} %get-tuple-element.51), channel_id=1, source_target_pairs={{64,0},{128,64},{192,128},{65,1},{129,65},{193,129},{66,2},{130,66... | collective-permute-start | bytes 49160 | tf_op jit(solution)/shard_map/ppermute | solution.py:33
  940.4 109.5 %reduce-scatter.15.cloned.1.call-done = f32[64,4]{1,0:T(8,128)} async-done(((f32[4096,4]{1,0:T(8,128)}), f32[64,4]{1,0:T(8,128)}) %reduce-scatter.15.cloned.1.call-update) | async-done | bytes 1040
  1050.9 54.8 %collective-permute-start.3 = (f32[2,64]{1,0:T(2,128)S(1)}, f32[2,64]{1,0:T(2,128)S(1)}, u32[]{:S(2)}, u32[]{:S(2)}) collective-permute-start(f32[2,64]{1,0:T(2,128)S(1)} %bitcast.152), channel_id=1, source_target_pairs={{0,64},{64,128},{128,192},{1,65},{65,129},{129,193},{2,66},{66,130... | collective-permute-start | bytes 1544 | tf_op jit(solution)/shard_map/ppermute | solution.py:33
  1114.4 74.8 %all-reduce.1 = (f32[2,800]{1,0:T(2,128)}, bf16[2,800]{1,0:T(2,128)(2,1)}) all-reduce(f32[2,800]{1,0:T(2,128)S(1)} %fusion.46, f32[2,800]{1,0:T(2,128)S(1)} %copy-done.17), channel_id=1, replica_groups=mesh['sym'=4,'dev'=64] {'sym','dev'}, use_global_device_ids=true, to_apply=%region_12.13 | all-reduce | flops 3200 | bytes 22400 | tf_op jit(solution)/shard_map/psum | solution.py:95
  1203.4 5.4 reshape.150
  1208.9 179.7 %all_gather.14 = bf16[2,2,4096]{1,0,2:T(2,128)(2,1)} all-gather(bf16[2,2,64]{1,0,2:T(2,128)(2,1)S(1)} %copy.69), channel_id=1, replica_groups=mesh['sym'=4,'dev'=64] {'dev'}, dimensions={2}, use_global_device_ids=true | all-gather | bytes 33280 | tf_op jit(solution)/shard_map/all_gather | solution.py:104
  1388.6 4.8 copy.70
  1394.1 26.0 %collective-permute-start.6 = (bf16[2,4096]{1,0:T(2,128)(2,1)}, bf16[2,4096]{1,0:T(2,128)(2,1)}, u32[]{:S(2)}, u32[]{:S(2)}) collective-permute-start(bf16[2,4096]{1,0:T(2,128)(2,1)} %get-tuple-element.49), channel_id=1, source_target_pairs={{64,0},{128,64},{192,128},{65,1},{129,65},{193,129},{66,2},{130,66... | collective-permute-start | bytes 49160 | tf_op jit(solution)/shard_map/ppermute | solution.py:33
  1426.3 109.4 %reduce-scatter.17.cloned.1.call-done = f32[64,4]{1,0:T(8,128)} async-done(((f32[4096,4]{1,0:T(8,128)}), f32[64,4]{1,0:T(8,128)}) %reduce-scatter.17.cloned.1.call-update) | async-done | bytes 1040
  1536.6 54.9 %collective-permute-start.7 = (f32[2,64]{1,0:T(2,128)S(1)}, f32[2,64]{1,0:T(2,128)S(1)}, u32[]{:S(2)}, u32[]{:S(2)}) collective-permute-start(f32[2,64]{1,0:T(2,128)S(1)} %bitcast.153), channel_id=1, source_target_pairs={{0,64},{64,128},{128,192},{1,65},{65,129},{129,193},{2,66},{66,130... | collective-permute-start | bytes 1544 | tf_op jit(solution)/shard_map/ppermute | solution.py:33
  1599.6 74.6 %all-reduce = (bf16[2,800]{1,0:T(2,128)(2,1)}, f32[2,800]{1,0:T(2,128)}) all-reduce(f32[2,800]{1,0:T(2,128)S(1)} %copy-done.16, f32[2,800]{1,0:T(2,128)S(1)} %fusion.47), channel_id=1, replica_groups=mesh['sym'=4,'dev'=64] {'sym','dev'}, use_global_device_ids=true, to_apply=%region_13.14 | all-reduce | flops 3200 | bytes 22400 | tf_op jit(solution)/shard_map/psum | solution.py:95
  1684.4 5.4 reshape.152
  1689.9 179.7 %all_gather.15 = bf16[2,2,4096]{1,0,2:T(2,128)(2,1)} all-gather(bf16[2,2,64]{1,0,2:T(2,128)(2,1)S(1)} %copy.77), channel_id=1, replica_groups=mesh['sym'=4,'dev'=64] {'dev'}, dimensions={2}, use_global_device_ids=true | all-gather | bytes 33280 | tf_op jit(solution)/shard_map/all_gather | solution.py:104
  1869.6 4.8 copy.78
  1874.5 26.1 %collective-permute-start.10 = (bf16[2,4096]{1,0:T(2,128)(2,1)S(1)}, bf16[2,4096]{1,0:T(2,128)(2,1)S(1)}, u32[]{:S(2)}, u32[]{:S(2)}) collective-permute-start(bf16[2,4096]{1,0:T(2,128)(2,1)S(1)} %get-tuple-element.47), channel_id=1, source_target_pairs={{64,0},{128,64},{192,128},{65,1},{129,65},{193,129},{66,2},{130,66... | collective-permute-start | bytes 49160 | tf_op jit(solution)/shard_map/ppermute | solution.py:33
  1904.3 112.6 %reduce-scatter.19.cloned.1.call-done = f32[64,4]{1,0:T(8,128)} async-done(((f32[4096,4]{1,0:T(8,128)}), f32[64,4]{1,0:T(8,128)}) %reduce-scatter.19.cloned.1.call-update) | async-done | bytes 1040
  2017.9 54.1 %collective-permute-start.11 = (f32[2,64]{1,0:T(2,128)S(1)}, f32[2,64]{1,0:T(2,128)S(1)}, u32[]{:S(2)}, u32[]{:S(2)}) collective-permute-start(f32[2,64]{1,0:T(2,128)S(1)} %bitcast.154), channel_id=1, source_target_pairs={{0,64},{64,128},{128,192},{1,65},{65,129},{129,193},{2,66},{66,130... | collective-permute-start | bytes 1544 | tf_op jit(solution)/shard_map/ppermute | solution.py:33
  (212 shorter events, 110.8 us)
Async XLA Ops:
  7.2 330.0 %copy-start = (bf16[800,800]{1,0:T(8,128)(2,1)S(1)}, bf16[800,800]{1,0:T(8,128)(2,1)}, u32[]{:S(2)}) copy-start(bf16[800,800]{1,0:T(8,128)(2,1)} %param.17) | copy-start | bytes 3840004
  7.2 553.4 %reduce-scatter.13.cloned.1.call-start = ((), (), s32[]{:S(2)}) async-start(), calls=%async_computation.4 | async-start | bytes 2129920
  197.2 429.1 %collective-permute-start = (bf16[2,4096]{1,0:T(2,128)(2,1)}, bf16[2,4096]{1,0:T(2,128)(2,1)}, u32[]{:S(2)}, u32[]{:S(2)}) collective-permute-start(bf16[2,4096]{1,0:T(2,128)(2,1)} %get-tuple-element.53), channel_id=1, source_target_pairs={{64,0},{128,64},{192,128},{65,1},{129,65},{193,129},{66,2},{130,66... | collective-permute-start | bytes 49160 | tf_op jit(solution)/shard_map/ppermute | solution.py:33
  237.8 812.1 %reduce-scatter.15.cloned.1.call-start = ((), (), s32[]{:S(2)}) async-start(), calls=%async_computation.5 | async-start | bytes 2129920
  242.2 92.5 %collective-permute-start.4 = (f32[2,800,1]{1,0,2:T(2,128)S(1)}, f32[2,800,1]{1,0,2:T(2,128)S(1)}, u32[]{:S(2)}, u32[]{:S(2)}) collective-permute-start(f32[2,800,1]{1,0,2:T(2,128)S(1)} %copy.101), channel_id=1, source_target_pairs={{0,1},{1,2},{2,3},{3,4},{4,5},{5,6},{6,7},{7,8},{8,9},{9,10},{10,1... | collective-permute-start | bytes 19208 | tf_op jit(solution)/shard_map/ppermute | solution.py:22
  245.5 90.4 %collective-permute-start.5 = (f32[2,800,1]{1,0,2:T(2,128)S(1)}, f32[2,800,1]{1,0,2:T(2,128)S(1)}, u32[]{:S(2)}, u32[]{:S(2)}) collective-permute-start(f32[2,800,1]{1,0,2:T(2,128)S(1)} %copy.67), channel_id=1, source_target_pairs={{1,0},{2,1},{3,2},{4,3},{5,4},{6,5},{7,6},{8,7},{9,8},{10,9},{11,1... | collective-permute-start | bytes 19208 | tf_op jit(solution)/shard_map/ppermute | solution.py:25
  258.9 80.9 %copy-start.32 = (bf16[2,800]{1,0:T(2,128)(2,1)}, bf16[2,800]{1,0:T(2,128)(2,1)S(1)}, u32[]{:S(2)}) copy-start(bf16[2,800]{1,0:T(2,128)(2,1)S(1)} %get-tuple-element.54) | copy-start | bytes 9604
  345.3 279.1 %collective-permute-start.9 = (f32[2,800,1]{1,0,2:T(2,128)}, f32[2,800,1]{1,0,2:T(2,128)}, u32[]{:S(2)}, u32[]{:S(2)}) collective-permute-start(f32[2,800,1]{1,0,2:T(2,128)} %copy.75), channel_id=1, source_target_pairs={{1,0},{2,1},{3,2},{4,3},{5,4},{6,5},{7,6},{8,7},{9,8},{10,9},{11,1... | collective-permute-start | bytes 19208 | tf_op jit(solution)/shard_map/ppermute | solution.py:25
  561.6 64.7 %collective-permute-start.1 = (f32[2,64]{1,0:T(2,128)S(1)}, f32[2,64]{1,0:T(2,128)S(1)}, u32[]{:S(2)}, u32[]{:S(2)}) collective-permute-start(f32[2,64]{1,0:T(2,128)S(1)} %bitcast.151), channel_id=1, source_target_pairs={{0,64},{64,128},{128,192},{1,65},{65,129},{129,193},{2,66},{66,130... | collective-permute-start | bytes 1544 | tf_op jit(solution)/shard_map/ppermute | solution.py:33
  622.3 81.1 %collective-permute-start.8 = (f32[2,800,1]{1,0,2:T(2,128)S(1)}, f32[2,800,1]{1,0,2:T(2,128)}, u32[]{:S(2)}, u32[]{:S(2)}) collective-permute-start(f32[2,800,1]{1,0,2:T(2,128)S(1)} %copy.73), channel_id=1, source_target_pairs={{0,1},{1,2},{2,3},{3,4},{4,5},{5,6},{6,7},{7,8},{8,9},{9,10},{10,1... | collective-permute-start | bytes 19208 | tf_op jit(solution)/shard_map/ppermute | solution.py:22
  626.4 78.9 %copy-start.15 = (f32[800]{0:T(1024)S(1)}, f32[800]{0:T(1024)}, u32[]{:S(2)}) copy-start(f32[800]{0:T(1024)} %get-tuple-element.57) | copy-start | bytes 9604
  723.0 812.7 %reduce-scatter.17.cloned.1.call-start = ((), (), s32[]{:S(2)}) async-start(), calls=%async_computation.6 | async-start | bytes 2129920
  908.0 204.1 %collective-permute-start.2 = (bf16[2,4096]{1,0:T(2,128)(2,1)}, bf16[2,4096]{1,0:T(2,128)(2,1)}, u32[]{:S(2)}, u32[]{:S(2)}) collective-permute-start(bf16[2,4096]{1,0:T(2,128)(2,1)} %get-tuple-element.51), channel_id=1, source_target_pairs={{64,0},{128,64},{192,128},{65,1},{129,65},{193,129},{66,2},{130,66... | collective-permute-start | bytes 49160 | tf_op jit(solution)/shard_map/ppermute | solution.py:33
  936.3 173.8 %collective-permute-start.13 = (f32[2,800,1]{1,0,2:T(2,128)}, f32[2,800,1]{1,0,2:T(2,128)}, u32[]{:S(2)}, u32[]{:S(2)}) collective-permute-start(f32[2,800,1]{1,0,2:T(2,128)} %copy.83), channel_id=1, source_target_pairs={{1,0},{2,1},{3,2},{4,3},{5,4},{6,5},{7,6},{8,7},{9,8},{10,9},{11,1... | collective-permute-start | bytes 19208 | tf_op jit(solution)/shard_map/ppermute | solution.py:25
  1050.9 61.2 %collective-permute-start.3 = (f32[2,64]{1,0:T(2,128)S(1)}, f32[2,64]{1,0:T(2,128)S(1)}, u32[]{:S(2)}, u32[]{:S(2)}) collective-permute-start(f32[2,64]{1,0:T(2,128)S(1)} %bitcast.152), channel_id=1, source_target_pairs={{0,64},{64,128},{128,192},{1,65},{65,129},{129,193},{2,66},{66,130... | collective-permute-start | bytes 1544 | tf_op jit(solution)/shard_map/ppermute | solution.py:33
  1108.0 81.2 %collective-permute-start.12 = (f32[2,800,1]{1,0,2:T(2,128)S(1)}, f32[2,800,1]{1,0,2:T(2,128)}, u32[]{:S(2)}, u32[]{:S(2)}) collective-permute-start(f32[2,800,1]{1,0,2:T(2,128)S(1)} %copy.81), channel_id=1, source_target_pairs={{0,1},{1,2},{2,3},{3,4},{4,5},{5,6},{6,7},{7,8},{8,9},{9,10},{10,1... | collective-permute-start | bytes 19208 | tf_op jit(solution)/shard_map/ppermute | solution.py:22
  1112.1 79.0 %copy-start.14 = (f32[800]{0:T(1024)S(1)}, f32[800]{0:T(1024)}, u32[]{:S(2)}) copy-start(f32[800]{0:T(1024)} %get-tuple-element.58) | copy-start | bytes 9604
  1208.8 808.1 %reduce-scatter.19.cloned.1.call-start = ((), (), s32[]{:S(2)}) async-start(), calls=%async_computation.7 | async-start | bytes 2129920
  1394.1 203.9 %collective-permute-start.6 = (bf16[2,4096]{1,0:T(2,128)(2,1)}, bf16[2,4096]{1,0:T(2,128)(2,1)}, u32[]{:S(2)}, u32[]{:S(2)}) collective-permute-start(bf16[2,4096]{1,0:T(2,128)(2,1)} %get-tuple-element.49), channel_id=1, source_target_pairs={{64,0},{128,64},{192,128},{65,1},{129,65},{193,129},{66,2},{130,66... | collective-permute-start | bytes 49160 | tf_op jit(solution)/shard_map/ppermute | solution.py:33
  1422.2 173.8 %collective-permute-start.15 = (f32[2,800,1]{1,0,2:T(2,128)}, f32[2,800,1]{1,0,2:T(2,128)}, u32[]{:S(2)}, u32[]{:S(2)}) collective-permute-start(f32[2,800,1]{1,0,2:T(2,128)} %copy.87), channel_id=1, source_target_pairs={{1,0},{2,1},{3,2},{4,3},{5,4},{6,5},{7,6},{8,7},{9,8},{10,9},{11,1... | collective-permute-start | bytes 19208 | tf_op jit(solution)/shard_map/ppermute | solution.py:25
  1536.6 61.3 %collective-permute-start.7 = (f32[2,64]{1,0:T(2,128)S(1)}, f32[2,64]{1,0:T(2,128)S(1)}, u32[]{:S(2)}, u32[]{:S(2)}) collective-permute-start(f32[2,64]{1,0:T(2,128)S(1)} %bitcast.153), channel_id=1, source_target_pairs={{0,64},{64,128},{128,192},{1,65},{65,129},{129,193},{2,66},{66,130... | collective-permute-start | bytes 1544 | tf_op jit(solution)/shard_map/ppermute | solution.py:33
  1593.9 80.4 %collective-permute-start.14 = (f32[2,800,1]{1,0,2:T(2,128)S(1)}, f32[2,800,1]{1,0,2:T(2,128)}, u32[]{:S(2)}, u32[]{:S(2)}) collective-permute-start(f32[2,800,1]{1,0,2:T(2,128)S(1)} %copy.85), channel_id=1, source_target_pairs={{0,1},{1,2},{2,3},{3,4},{4,5},{5,6},{6,7},{7,8},{8,9},{9,10},{10,1... | collective-permute-start | bytes 19208 | tf_op jit(solution)/shard_map/ppermute | solution.py:22
  1874.5 197.8 %collective-permute-start.10 = (bf16[2,4096]{1,0:T(2,128)(2,1)S(1)}, bf16[2,4096]{1,0:T(2,128)(2,1)S(1)}, u32[]{:S(2)}, u32[]{:S(2)}) collective-permute-start(bf16[2,4096]{1,0:T(2,128)(2,1)S(1)} %get-tuple-element.47), channel_id=1, source_target_pairs={{64,0},{128,64},{192,128},{65,1},{129,65},{193,129},{66,2},{130,66... | collective-permute-start | bytes 49160 | tf_op jit(solution)/shard_map/ppermute | solution.py:33
  1900.6 171.4 %copy-start.33 = (bf16[2,800]{1,0:T(2,128)(2,1)S(1)}, bf16[2,800]{1,0:T(2,128)(2,1)}, u32[]{:S(2)}) copy-start(bf16[2,800]{1,0:T(2,128)(2,1)} %copy-done.32) | copy-start | bytes 9604
  1900.6 171.4 %copy-start.39 = (bf16[2,800]{1,0:T(2,128)(2,1)S(1)}, bf16[2,800]{1,0:T(2,128)(2,1)}, u32[]{:S(2)}) copy-start(bf16[2,800]{1,0:T(2,128)(2,1)} %get-tuple-element.2) | copy-start | bytes 9604
  1903.8 168.9 %copy-start.21 = (pred[2,64]{1,0:T(4,128)(4,1)S(1)}, pred[2,64]{1,0:T(4,128)(4,1)}, u32[]{:S(2)}) copy-start(pred[2,64]{1,0:T(4,128)(4,1)} %copy-done.19) | copy-start | bytes 388
  1903.8 169.3 %copy-start.23 = (f32[2,1,64]{2,1,0:T(1,128)S(1)}, f32[2,1,64]{2,1,0:T(1,128)}, u32[]{:S(2)}) copy-start(f32[2,1,64]{2,1,0:T(1,128)} %copy-done.22) | copy-start | bytes 1540
  1903.8 169.3 %copy-start.25 = (f32[2,1,64]{2,1,0:T(1,128)S(1)}, f32[2,1,64]{2,1,0:T(1,128)}, u32[]{:S(2)}) copy-start(f32[2,1,64]{2,1,0:T(1,128)} %copy-done.24) | copy-start | bytes 1540
  1903.9 169.3 %copy-start.27 = (f32[2,1,64]{2,1,0:T(1,128)S(1)}, f32[2,1,64]{2,1,0:T(1,128)}, u32[]{:S(2)}) copy-start(f32[2,1,64]{2,1,0:T(1,128)} %copy-done.26) | copy-start | bytes 1540
  1903.9 169.3 %copy-start.29 = (f32[2,1,64]{2,1,0:T(1,128)S(1)}, f32[2,1,64]{2,1,0:T(1,128)}, u32[]{:S(2)}) copy-start(f32[2,1,64]{2,1,0:T(1,128)} %copy-done.28) | copy-start | bytes 1540
  1903.9 169.3 %copy-start.30 = (f32[2,2,64]{2,1,0:T(2,128)S(1)}, f32[2,2,64]{2,1,0:T(2,128)}, u32[]{:S(2)}) copy-start(f32[2,2,64]{2,1,0:T(2,128)} %param.9) | copy-start | bytes 3076
  2017.9 54.8 %collective-permute-start.11 = (f32[2,64]{1,0:T(2,128)S(1)}, f32[2,64]{1,0:T(2,128)S(1)}, u32[]{:S(2)}, u32[]{:S(2)}) collective-permute-start(f32[2,64]{1,0:T(2,128)S(1)} %bitcast.154), channel_id=1, source_target_pairs={{0,64},{64,128},{128,192},{1,65},{65,129},{129,193},{2,66},{66,130... | collective-permute-start | bytes 1544 | tf_op jit(solution)/shard_map/ppermute | solution.py:33
  (28 other events, 376.2 us)
Sparse Core Ops, SparseCore 0:
  237.9 322.6 reduce-scatter.12
  723.1 326.7 reduce-scatter.14
  1208.9 326.6 reduce-scatter.16
  1690.0 326.8 reduce-scatter.18
where the time goes:
time: 2080 us
  blocking collectives  1020 us (49%)
  waiting for transfers between devices  540 us (26%)
  starting transfers between devices  358 us (17%)
  local copies, waits for them, and re-layouts  103 us (5%)
  matrix products  26.6 us (1%)
    all_gather x4, blocking collectives, on_device(): own_blocks = lax.all_gather(state_half, 'dev', axis=2, tiled=True)  721 us
    unnamed x8, waiting for transfers between devices  540 us
    ppermute x8, starting transfers between devices, shifted_2(): return lax.ppermute(block, axis, route)  329 us
    psum x4, blocking collectives, on_device(): lax.psum((boundary_part, slope_part), ('sym', 'dev'))  298 us
    unnamed x101, local copies, waits for them, and re-layouts  49.7 us
  transfers between devices with their start and end apart: 20, of which 5 were waited for; matrix products, arithmetic and copies ran while one was open for 4% of the time, Pallas kernels for 0%

commit v1 on v0

v1 whole, which is shorter than its diff:
```python
import functools

import jax
import jax.numpy as jnp
from jax import lax
from jax.experimental import pallas as pl
from jax.experimental.pallas import tpu as pltpu
from jax.sharding import PartitionSpec as P

TERMS = 4
time_step = 0.012
spacing = 0.1
kinetic = 0.5 / (spacing * spacing)
block_scale = 90.0
dipole_scale = 40.0
laser_scale = 25.0

MESH = pl.DeviceIdType.MESH
F32, BF16 = jnp.float32, jnp.bfloat16
NT = (((1,), (1,)), ((), ()))

SYM, DEV = 4, 64
TOP = 8


def torus(step):
    return min(step, 4 - step)


OFFSETS = sorted(
    [(oy, ox) for oy in range(4) for ox in range(4) if (oy, ox) != (0, 0)],
    key=lambda o: -(torus(o[0]) + torus(o[1])),
)


def remote(src, dst, send, recv, sym, dev):
    return pltpu.make_async_remote_copy(
        src_ref=src, dst_ref=dst, send_sem=send, recv_sem=recv, device_id=(sym, dev), device_id_type=MESH
    )


def drain(ref, sem):
    pltpu.make_async_copy(ref, ref, sem).wait()


def kernel(
    sizes, inner, ham, dip, amps, chan, outer, energy, laser,
    inner_out, outer_out,
    inn, mats, dips, ampv, chv, out_raw, env, lasv, u, acc, wst, wsum,
    stage1, got1, stage2, own, stage3, above, stage4, below,
    bst, bgot, bst2, bgot2, sgot,
    load, store, halo_send, halo_recv, send1, recv1, send2, recv2, send3, recv3, send4, recv4,
    bsend, brecv, bsend2, brecv2, ssend, srecv, ssend2,
):
    s = lax.axis_index("sym")
    d = lax.axis_index("dev")
    y, zl, x = d // 16, (d // 4) % 4, d % 4
    plane = y * 4 + x
    parity = x % 2
    group = s * 4 + zl
    is_plane_root = plane == 0
    is_root = jnp.logical_and(s == 0, d == 0)
    is_last = jnp.logical_and(s == SYM - 1, d == DEV - 1)
    channels = ampv.shape[1]
    points = out_raw.shape[2]
    rows = u.shape[1]

    def dev_of(y_, z_, x_):
        return (y_ * 4 + z_) * 4 + x_

    loads = [
        pltpu.make_async_copy(inner, inn, load.at[0]),
        pltpu.make_async_copy(dip, dips, load.at[1]),
        pltpu.make_async_copy(amps, ampv, load.at[2]),
        pltpu.make_async_copy(chan, chv, load.at[3]),
        pltpu.make_async_copy(outer, out_raw, load.at[4]),
        pltpu.make_async_copy(energy, env, load.at[5]),
        pltpu.make_async_copy(laser, lasv, load.at[6]),
        pltpu.make_async_copy(ham, mats, load.at[7]),
    ]
    for one in loads:
        one.start()

    barrier = pltpu.get_barrier_semaphore()

    def greet(sym, dev):
        pl.semaphore_signal(barrier, inc=1, device_id=(sym, dev), device_id_type=MESH)

    for oy, ox in OFFSETS:
        greet(s, dev_of((y + oy) % 4, zl, (x + ox) % 4))
    for oz in range(1, 4):
        greet(s, dev_of(y, (zl + oz) % 4, x))
    expected = jnp.int32(18)
    has_below = s > 0
    has_above = s < SYM - 1

    @pl.when(has_below)
    def _():
        for z_ in range(4):
            greet(s - 1, dev_of(y, z_, x))

    @pl.when(has_above)
    def _():
        for z_ in range(4):
            greet(s + 1, dev_of(y, z_, x))

    expected += 4 * has_below.astype(jnp.int32) + 4 * has_above.astype(jnp.int32)

    @pl.when(is_root)
    def _():
        for g in range(1, 16):
            greet(jnp.int32(g // 4), jnp.int32((g % 4) * 4))

    hears_root = jnp.logical_and(is_plane_root, jnp.logical_not(is_root))

    @pl.when(hears_root)
    def _():
        greet(jnp.int32(0), jnp.int32(0))

    expected += 15 * is_root.astype(jnp.int32) + hears_root.astype(jnp.int32)
    position = s * DEV + d
    left, right = position - 1, position + 1
    has_left = jnp.logical_not(is_root)
    has_right = jnp.logical_not(is_last)

    @pl.when(has_left)
    def _():
        greet(left // DEV, left % DEV)

    @pl.when(has_right)
    def _():
        greet(right // DEV, right % DEV)

    expected += has_left.astype(jnp.int32) + has_right.astype(jnp.int32)

    loads[0].wait()
    size0, size1 = sizes[2 * s], sizes[2 * s + 1]
    row_index = d * 64 + lax.broadcasted_iota(jnp.int32, (2, 64), 1)
    live0 = row_index < size0
    live1 = row_index < size1
    first = jnp.concatenate(
        [jnp.where(live0, inn[0], 0.0), jnp.where(live1, inn[1], 0.0)], axis=0
    )
    wst[...] = first
    wsum[...] = first
    for one in loads[2:6]:
        one.wait()
    blank = jnp.zeros((2, TOP, channels), F32)

    @pl.when(is_root)
    def _():
        u[:, 0:TOP, :] = blank

    @pl.when(is_last)
    def _():
        u[:, TOP + points : rows, :] = blank

    for i in range(2):
        turned = jnp.transpose(out_raw[i])
        u[i, TOP : TOP + points, :] = turned
        acc[i] = turned

    def slope_of(i):
        near = u[i, TOP : TOP + 8, :]
        return (-3.0 * near[0:1] + 4.0 * near[1:2] - near[2:3]) * (0.5 / spacing)

    def stage_slope(k):
        both = jnp.concatenate([slope_of(0), slope_of(1)], axis=0)
        sgot[k] = both.astype(BF16)

    @pl.when(is_root)
    def _():
        stage_slope(0)

    pl.semaphore_wait(barrier, expected)

    to_left = remote(
        u.at[:, pl.ds(TOP, 8), :], u.at[:, pl.ds(TOP + points, 8), :],
        halo_send.at[0], halo_recv.at[0], left // DEV, left % DEV,
    )
    to_right = remote(
        u.at[:, pl.ds(points, 8), :], u.at[:, pl.ds(0, 8), :],
        halo_send.at[1], halo_recv.at[1], right // DEV, right % DEV,
    )

    @pl.when(has_left)
    def _():
        to_left.start()

    @pl.when(has_right)
    def _():
        to_right.start()

    loads[1].wait()
    owned0 = (chv[...] == 2 * s).astype(F32)
    owned1 = (chv[...] == 2 * s + 1).astype(F32)
    zero64 = jnp.zeros((2, 64), BF16)
    line = lax.broadcasted_iota(jnp.int32, (rows, 1), 0)
    inside = jnp.logical_and(
        jnp.logical_or(line >= TOP, has_left), jnp.logical_or(line < TOP + points, has_right)
    )

    def slope_to(k, g):
        return remote(
            sgot.at[k], sgot.at[k], ssend.at[g], srecv.at[k], jnp.int32(g // 4), jnp.int32((g % 4) * 4)
        )

    def slope_on(k, n):
        oy, ox = OFFSETS[n]
        return remote(sgot.at[k], sgot.at[k], ssend2.at[n], srecv.at[k], s, dev_of(oy, zl, ox))

    @pl.loop(0, TERMS)
    def _(k):
        factor = time_step / (k + 1).astype(F32)
        half = wst[...].astype(BF16)

        spread = jnp.concatenate(
            [jnp.concatenate([half[0:2], zero64], axis=1), jnp.concatenate([zero64, half[2:4]], axis=1)], axis=0
        )
        flat = dips[...].reshape(128, dips.shape[2])
        part = jnp.dot(spread, flat, preferred_element_type=F32).astype(BF16)
        zero4 = jnp.zeros((4, 64), BF16)
        even = jnp.concatenate([half, zero4], axis=1)
        odd = jnp.concatenate([zero4, half], axis=1)
        chunk = jnp.where(parity == 0, even, odd)
        for y_ in range(4):
            for xh in range(2):
                stage1[y_ * 2 + xh, 0] = chunk
                for z_ in range(4):
                    tile = (y_ * 4 + z_) * 2 + xh
                    stage1[y_ * 2 + xh, 1 + z_] = part[:, tile * 128 : (tile + 1) * 128]
        sends1 = []
        for n, (oy, ox) in enumerate(OFFSETS):
            ty, tx = (y + oy) % 4, (x + ox) % 4
            sends1.append(
                remote(
                    stage1.at[ty * 2 + tx // 2], got1.at[k, plane], send1, recv1.at[k], s, dev_of(ty, zl, tx)
                )
            )
            sends1[-1].start()

        @pl.when(is_root)
        def _():
            for g in range(1, 16):
                slope_to(k, g).start()

        per_block = jnp.dot(half, ampv[...], preferred_element_type=F32)
        bound = owned0 * per_block[0:2] + owned1 * per_block[2:4]

        @pl.when(is_plane_root)
        def _():
            bgot[k, 0] = bound

        @pl.when(jnp.logical_not(is_plane_root))
        def _():
            bst[...] = bound
            remote(bst, bgot.at[k, plane], bsend, brecv.at[k], s, dev_of(0, zl, 0)).start()

        got1[k, plane] = stage1[y * 2 + x // 2]
        drain(got1.at[k, pl.ds(0, 15)], recv1.at[k])

        sums = got1[k, 0, 1:5].astype(F32)
        for p in range(1, 16):
            sums += got1[k, p, 1:5].astype(F32)
        sums = sums.astype(BF16)
        pairs = [got1[k, 2 * q, 0] + got1[k, 2 * q + 1, 0] for q in range(8)]
        for z_ in range(4):
            for q in range(8):
                stage2[z_, q] = pairs[q]
            stage2[z_, 8] = sums[z_]
            stage4[z_] = sums[z_]
        for q in range(8):
            stage3[q] = pairs[q][0:2]
        for oz in (2, 1, 3):
            tz = (zl + oz) % 4
            remote(stage2.at[tz], own.at[k, zl], send2, recv2.at[k], s, dev_of(y, tz, x)).start()

        @pl.when(has_below)
        def _():
            for z_ in range(4):
                remote(stage3, above.at[k, zl], send3, recv3.at[k], s - 1, dev_of(y, z_, x)).start()

        @pl.when(has_above)
        def _():
            for z_ in range(4):
                remote(stage4.at[z_], below.at[k, zl], send4, recv4.at[k], s + 1, dev_of(y, z_, x)).start()

        own[k, zl] = stage2[zl]

        @pl.when(is_plane_root)
        def _():
            drain(bgot.at[k, pl.ds(0, 15)], brecv.at[k])
            total = jnp.sum(bgot[k], axis=0)

            @pl.when(is_root)
            def _():
                bgot2[k, 0] = total

            @pl.when(jnp.logical_not(is_root))
            def _():
                bst2[...] = total
                remote(bst2, bgot2.at[k, group], bsend2, brecv2.at[k], jnp.int32(0), jnp.int32(0)).start()
                drain(sgot.at[k], srecv.at[k])

            for n in range(15):
                slope_on(k, n).start()

        @pl.when(k == 0)
        def _():
            @pl.when(has_left)
            def _():
                to_right.wait_recv()
                to_left.wait_send()

            @pl.when(has_right)
            def _():
                to_left.wait_recv()
                to_right.wait_send()

            loads[6].wait()
            loads[7].wait()

        images = []
        for i in range(2):
            value = u[i]
            mixed = jnp.dot(value.astype(BF16), lasv[...], preferred_element_type=F32)
            curve = pltpu.roll(value, 1, 0) - 2.0 * value + pltpu.roll(value, rows - 1, 0)
            image = -kinetic * curve + env[...] * value + laser_scale * mixed
            images.append(jnp.where(inside, image, 0.0))
        new0 = factor * images[1]
        new1 = -factor * images[0]
        u[0] = new0
        u[1] = new1
        acc[0] += new0[TOP : TOP + points]
        acc[1] += new1[TOP : TOP + points]

        @pl.when(jnp.logical_not(is_plane_root))
        def _():
            drain(sgot.at[k], srecv.at[k])

        slope = sgot[k].astype(F32)
        masked = jnp.concatenate([owned0 * slope, owned1 * slope], axis=0).astype(BF16)
        bloch = lax.dot_general(masked, ampv[...], NT, preferred_element_type=F32)

        drain(own.at[k, pl.ds(0, 3)], recv2.at[k])

        @pl.when(has_above)
        def _():
            drain(above.at[k], recv3.at[k])

        @pl.when(has_below)
        def _():
            drain(below.at[k], recv4.at[k])

        order = [(y_, z_, xh) for y_ in range(4) for z_ in range(4) for xh in range(2)]
        mine = jnp.concatenate([own[k, z_, y_ * 2 + xh] for y_, z_, xh in order], axis=1)
        upper = jnp.concatenate([above[k, z_, y_ * 2 + xh] for y_, z_, xh in order], axis=1)

        def times(vectors, matrix):
            return lax.dot_general(vectors, matrix, NT, preferred_element_type=F32)

        diag0 = times(mine, mats[0])[0:2]
        diag1 = times(mine, mats[1])[2:4]
        forward0 = times(mine, dips[0])[2:4]
        forward1 = jnp.where(has_above, times(upper, dips[1]), 0.0)

        def half_of(tile):
            return jnp.where(parity == 0, tile[:, 0:64], tile[:, 64:128])

        lower0 = below[k, 0].astype(F32)
        lower1 = own[k, 0, 8].astype(F32)
        for z_ in range(1, 4):
            lower0 += below[k, z_].astype(F32)
            lower1 += own[k, z_, 8].astype(F32)
        lower0 = jnp.where(has_below, half_of(lower0)[2:4], 0.0)
        lower1 = half_of(lower1)[0:2]
        image0 = block_scale * diag0 + dipole_scale * (forward0 + lower0) + bloch[0:2]
        image1 = block_scale * diag1 + dipole_scale * (forward1 + lower1) + bloch[2:4]
        image0 = jnp.where(live0, image0, 0.0)
        image1 = jnp.where(live1, image1, 0.0)
        fresh = factor * jnp.concatenate([image0[1:2], -image0[0:1], image1[1:2], -image1[0:1]], axis=0)
        wst[...] = fresh
        wsum[...] += fresh

        @pl.when(is_root)
        def _():
            drain(bgot2.at[k, pl.ds(0, 15)], brecv2.at[k])
            edge = (-kinetic) * jnp.sum(bgot2[k], axis=0)
            fix0 = factor * edge[1:2]
            fix1 = -factor * edge[0:1]
            u[0, TOP : TOP + 1, :] += fix0
            u[1, TOP : TOP + 1, :] += fix1
            acc[0, 0:1, :] += fix0
            acc[1, 0:1, :] += fix1

            @pl.when(k < TERMS - 1)
            def _():
                stage_slope(k + 1)

        drain(got1.at[k, pl.ds(0, 15)], send1)
        drain(own.at[k, pl.ds(0, 3)], send2)

        @pl.when(has_below)
        def _():
            drain(above.at[k], send3)

        @pl.when(has_above)
        def _():
            drain(below.at[k], send4)

        @pl.when(jnp.logical_not(is_plane_root))
        def _():
            drain(bst, bsend)

        @pl.when(is_plane_root)
        def _():
            for n in range(15):
                slope_on(k, n).wait_send()

        @pl.when(is_root)
        def _():
            for g in range(1, 16):
                slope_to(k, g).wait_send()

        @pl.when(hears_root)
        def _():
            drain(bst2, bsend2)

    inner_out[0] = wsum[0:2]
    inner_out[1] = wsum[2:4]
    for i in range(2):
        out_raw[i] = jnp.transpose(acc[i])
    last = pltpu.make_async_copy(out_raw, outer_out, store)
    last.start()
    last.wait()


def on_device(inner, sizes, ham, dip, amps, chan, outer, energy, laser):
    blocks, parts, own_rows = inner.shape
    states = ham.shape[2]
    channels, points = outer.shape[1], outer.shape[2]
    rows = points + 16
    dma = pltpu.SemaphoreType.DMA
    anywhere = pl.BlockSpec(memory_space=pl.ANY)
    return pl.pallas_call(
        kernel,
        out_shape=(
            jax.ShapeDtypeStruct(inner.shape, F32),
            jax.ShapeDtypeStruct(outer.shape, F32),
        ),
        in_specs=[pl.BlockSpec(memory_space=pltpu.SMEM)] + [anywhere] * 8,
        out_specs=(pl.BlockSpec(memory_space=pltpu.VMEM), anywhere),
        scratch_shapes=[
            pltpu.VMEM(inner.shape, F32),
            pltpu.VMEM(ham.shape, BF16),
            pltpu.VMEM(dip.shape, BF16),
            pltpu.VMEM((own_rows, channels), BF16),
            pltpu.VMEM((1, channels), jnp.int32),
            pltpu.VMEM(outer.shape, F32),
            pltpu.VMEM((1, channels), F32),
            pltpu.VMEM(laser.shape, BF16),
            pltpu.VMEM((2, rows, channels), F32),
            pltpu.VMEM((2, points, channels), F32),
            pltpu.VMEM((4, own_rows), F32),
            pltpu.VMEM((4, own_rows), F32),
            pltpu.VMEM((8, 5, 4, 128), BF16),
            pltpu.VMEM((TERMS, 16, 5, 4, 128), BF16),
            pltpu.VMEM((4, 9, 4, 128), BF16),
            pltpu.VMEM((TERMS, 4, 9, 4, 128), BF16),
            pltpu.VMEM((8, 2, 128), BF16),
            pltpu.VMEM((TERMS, 4, 8, 2, 128), BF16),
            pltpu.VMEM((4, 4, 128), BF16),
            pltpu.VMEM((TERMS, 4, 4, 128), BF16),
            pltpu.VMEM((2, channels), F32),
            pltpu.VMEM((TERMS, 16, 2, channels), F32),
            pltpu.VMEM((2, channels), F32),
            pltpu.VMEM((TERMS, 16, 2, channels), F32),
            pltpu.VMEM((TERMS, 2, channels), BF16),
            dma((8,)), dma, dma((2,)), dma((2,)),
            dma, dma((TERMS,)), dma, dma((TERMS,)), dma, dma((TERMS,)), dma, dma((TERMS,)),
            dma, dma((TERMS,)), dma, dma((TERMS,)), dma((16,)), dma((TERMS,)), dma((15,)),
        ],
        compiler_params=pltpu.CompilerParams(
            collective_id=0, has_side_effects=True, vmem_limit_bytes=60 * 1024 * 1024
        ),
    )(
        sizes, inner, ham, dip, amps.T, chan.reshape(1, channels), outer, energy.reshape(1, channels), laser,
    )


def solution(mesh):
    placed = (
        P("sym", None, "dev"),
        P(),
        P("sym", "dev", None),
        P("sym", "dev", None),
        P(None, "dev"),
        P(),
        P(None, None, ("sym", "dev")),
        P(),
        P(),
    )
    return jax.shard_map(
        on_device,
        mesh=mesh,
        in_specs=placed,
        out_specs=(P("sym", None, "dev"), P(None, None, ("sym", "dev"))),
        check_vma=False,
    )
```

time: 2080 us -> 63.4 us (0.03)
  blocking collectives: 1020 us -> 0 us
  waiting for transfers between devices: 540 us -> 0 us
  starting transfers between devices: 358 us -> 0 us
  local copies, waits for them, and re-layouts: 103 us -> 4.6 us
  Pallas kernels: 0 us -> 58 us
  matrix products: 26.6 us -> 0 us
    all_gather x4 -> x0, blocking collectives: 721 us -> none  [on_device(): own_blocks = lax.all_gather(state_half, 'dev', axis=2, tiled=True)]
    unnamed x8 -> x0, waiting for transfers between devices: 540 us -> none
    ppermute x16 -> x0, starting transfers between devices: 358 us -> none  [the longest x8 329 us: shifted_2(): return lax.ppermute(block, axis, route)]
    psum x4 -> x0, blocking collectives: 298 us -> none  [on_device(): lax.psum((boundary_part, slope_part), ('sym', 'dev'))]
    pallas_call x0 -> x1, Pallas kernels: none -> 58 us  [on_device(): pl.pallas_call(kernel, out_shape=(jax.ShapeDtypeStruct(inner.shape, F32),...]
    unnamed x101 -> x2, local copies, waits for them, and re-layouts: 49.7 us -> 3.33 us
    dot_general x24 -> x0, matrix products: 26.6 us -> none  [the longest x4 11.8 us: outer_local(): jnp.einsum('cd,idn->icn', laser_dipole, values.astype(jnp.bfloat16), pref...]
    slice x19 -> x0, local copies, waits for them, and re-layouts: 21.1 us -> none  [the longest x4 7.54 us: on_device(): real_cells[:, :, 0]]
  transfers between devices with their start and end apart: 20 -> 0, of which waited for: 5 -> 0; matrix products, arithmetic and copies ran while one was open for 4% -> 0% of each run, Pallas kernels for 0% -> 0%
where the time goes in v1:
time: 63.4 us; the launch traced here: 63.2 us
  Pallas kernels  58 us (91%)
  local copies, waits for them, and re-layouts  4.6 us (7%)
  between operations  0.64 us (1%)
    pallas_call x1, Pallas kernels, on_device(): pl.pallas_call(kernel, out_shape=(jax.ShapeDtypeStruct(inner.shape, F32),...  58 us
    unnamed x2, local copies, waits for them, and re-layouts  3.33 us
    reshape x1, local copies, waits for them, and re-layouts, on_device(): energy.reshape(1, channels)  1.27 us

profile of v1, /device:TPU:1, one launch (start us, length us, event | category | flops | bytes accessed | tf_op | source)
XLA Modules:
  0.0 63.2 jit_solution(17988336597039644549)
XLA Ops:
  0.6 1.3 %reshape.11.energy = f32[1,800]{1,0:T(1,128)} reshape(f32[800]{0:T(1024)} %param.16) | data formatting | bytes 6400 | tf_op jit(solution)/shard_map/reshape | solution.py:487
  1.9 58.0 %shard_map.104 = (f32[2,2,64]{2,1,0:T(2,128)}, f32[2,800,128]{2,1,0:T(8,128)}) custom-call(s32[8]{0:T(128)} %sizes.1, f32[2,2,64]{2,1,0:T(2,128)} %inner.1, bf16[2,64,4096]{2,1,0:T(8,128)(2,1)} %ham.1, bf16[2,64,4096]{2,1,0:T(8,128)(2,1)} %dip.1, bf16[64,800]{1,0:T(8,128)(2,1)} %bitcast.2, s32[1,800]{1,0:T(1,128)} %bitcast.3, f32[2,800,128]{2,1,0:T(8,128)} %outer.1, ...), custom_call_target="tpu_custom_call" | custom-call | tf_op jit(solution)/shard_map/pallas_call | solution.py:445
  59.9 1.2 %copy.13 = f32[2,2,64]{2,1,0:T(2,128)} copy(f32[2,2,64]{2,1,0:T(2,128)} %get-tuple-element.4) | data formatting | bytes 2048
  61.1 2.1 %copy.14 = f32[2,800,128]{2,1,0:T(8,128)} copy(f32[2,800,128]{2,1,0:T(8,128)} %get-tuple-element.5) | data formatting | bytes 1638400

commit v2 on v1

v2 whole, which is shorter than its diff:
```python
import functools

import jax
import jax.numpy as jnp
from jax import lax
from jax.experimental import pallas as pl
from jax.experimental.pallas import tpu as pltpu
from jax.sharding import PartitionSpec as P

TERMS = 4
time_step = 0.012
spacing = 0.1
kinetic = 0.5 / (spacing * spacing)
block_scale = 90.0
dipole_scale = 40.0
laser_scale = 25.0

MESH = pl.DeviceIdType.MESH
F32, BF16 = jnp.float32, jnp.bfloat16
NT = (((1,), (1,)), ((), ()))

SYM, DEV = 4, 64
TOP = 8


def torus(step):
    return min(step, 4 - step)


OFFSETS = sorted(
    [(oy, ox) for oy in range(4) for ox in range(4) if (oy, ox) != (0, 0)],
    key=lambda o: -(torus(o[0]) + torus(o[1])),
)


def remote(src, dst, send, recv, sym, dev):
    return pltpu.make_async_remote_copy(
        src_ref=src, dst_ref=dst, send_sem=send, recv_sem=recv, device_id=(sym, dev), device_id_type=MESH
    )


def drain(ref, sem):
    pltpu.make_async_copy(ref, ref, sem).wait()


def kernel(
    sizes_in, inner, ham, dip, amps, chan, outer, energy, laser,
    inner_out, outer_out,
    sizes, inn, mats, dips, ampv, chv, out_raw, env, lasv, u, acc, wsum,
    stage1, got1, stage2, own, stage3, above, stage4, below,
    bst, bgot, bst2, bgot2, sgot,
    load, halo_send, halo_recv, send1, recv1, send2, recv2, send3, recv3, send4, recv4,
    bsend, brecv, bsend2, brecv2, ssend, srecv, ssend2,
):
    s = lax.axis_index("sym")
    d = lax.axis_index("dev")
    y, zl, x = d // 16, (d // 4) % 4, d % 4
    plane = y * 4 + x
    parity = x % 2
    group = s * 4 + zl
    is_plane_root = plane == 0
    is_root = jnp.logical_and(s == 0, d == 0)
    is_last = jnp.logical_and(s == SYM - 1, d == DEV - 1)
    channels = ampv.shape[1]
    points = out_raw.shape[2]
    rows = u.shape[1]

    def dev_of(y_, z_, x_):
        return (y_ * 4 + z_) * 4 + x_

    barrier = pltpu.get_barrier_semaphore()

    def greet(sym, dev):
        pl.semaphore_signal(barrier, inc=1, device_id=(sym, dev), device_id_type=MESH)

    for oy, ox in OFFSETS:
        greet(s, dev_of((y + oy) % 4, zl, (x + ox) % 4))
    for oz in range(1, 4):
        greet(s, dev_of(y, (zl + oz) % 4, x))
    expected = jnp.int32(18)
    has_below = s > 0
    has_above = s < SYM - 1

    @pl.when(has_below)
    def _():
        for z_ in range(4):
            greet(s - 1, dev_of(y, z_, x))

    @pl.when(has_above)
    def _():
        for z_ in range(4):
            greet(s + 1, dev_of(y, z_, x))

    expected += 4 * has_below.astype(jnp.int32) + 4 * has_above.astype(jnp.int32)

    @pl.when(is_root)
    def _():
        for g in range(1, 16):
            greet(jnp.int32(g // 4), jnp.int32((g % 4) * 4))

    hears_root = jnp.logical_and(is_plane_root, jnp.logical_not(is_root))

    @pl.when(hears_root)
    def _():
        greet(jnp.int32(0), jnp.int32(0))

    expected += 15 * is_root.astype(jnp.int32) + hears_root.astype(jnp.int32)
    position = s * DEV + d
    left, right = position - 1, position + 1
    has_left = jnp.logical_not(is_root)
    has_right = jnp.logical_not(is_last)

    @pl.when(has_left)
    def _():
        greet(left // DEV, left % DEV)

    @pl.when(has_right)
    def _():
        greet(right // DEV, right % DEV)

    expected += has_left.astype(jnp.int32) + has_right.astype(jnp.int32)

    pairs = (
        (sizes_in, sizes), (inner, inn), (dip, dips), (amps, ampv), (chan, chv),
        (outer, out_raw), (energy, env), (laser, lasv), (ham, mats),
    )
    loads = [pltpu.make_async_copy(src, dst, load.at[n]) for n, (src, dst) in enumerate(pairs)]
    for one in loads:
        one.start()

    for one in loads[0:3]:
        one.wait()
    size0, size1 = sizes[2 * s], sizes[2 * s + 1]
    row_index = d * 64 + lax.broadcasted_iota(jnp.int32, (2, 64), 1)
    live0 = row_index < size0
    live1 = row_index < size1
    zero2 = jnp.zeros((2, 64), BF16)
    zero4 = jnp.zeros((4, 64), BF16)

    def prepare(state):
        half = state.astype(BF16)
        spread = jnp.concatenate(
            [jnp.concatenate([half[0:2], zero2], axis=1), jnp.concatenate([zero2, half[2:4]], axis=1)], axis=0
        )
        flat = dips[...].reshape(128, dips.shape[2])
        part = jnp.dot(spread, flat, preferred_element_type=F32).astype(BF16)
        even = jnp.concatenate([half, zero4], axis=1)
        odd = jnp.concatenate([zero4, half], axis=1)
        chunk = jnp.where(parity == 0, even, odd)
        for y_ in range(4):
            for xh in range(2):
                stage1[y_ * 2 + xh, 0] = chunk
                for z_ in range(4):
                    tile = (y_ * 4 + z_) * 2 + xh
                    stage1[y_ * 2 + xh, 1 + z_] = part[:, tile * 128 : (tile + 1) * 128]
        per_block = jnp.dot(half, ampv[...], preferred_element_type=F32)
        bst[...] = owned0 * per_block[0:2] + owned1 * per_block[2:4]

    first = jnp.concatenate(
        [jnp.where(live0, inn[0], 0.0), jnp.where(live1, inn[1], 0.0)], axis=0
    )
    wsum[...] = first
    loads[3].wait()
    loads[4].wait()
    owned0 = (chv[...] == 2 * s).astype(F32)
    owned1 = (chv[...] == 2 * s + 1).astype(F32)
    prepare(first)

    loads[5].wait()
    blank = jnp.zeros((2, TOP, channels), F32)

    @pl.when(is_root)
    def _():
        u[:, 0:TOP, :] = blank

    @pl.when(is_last)
    def _():
        u[:, TOP + points : rows, :] = blank

    for i in range(2):
        turned = jnp.transpose(out_raw[i])
        u[i, TOP : TOP + points, :] = turned
        acc[i] = turned

    def slope_of(i):
        near = u[i, TOP : TOP + 8, :]
        return (-3.0 * near[0:1] + 4.0 * near[1:2] - near[2:3]) * (0.5 / spacing)

    def stage_slope(k):
        both = jnp.concatenate([slope_of(0), slope_of(1)], axis=0)
        sgot[k] = both.astype(BF16)

    @pl.when(is_root)
    def _():
        stage_slope(0)

    for one in loads[6:9]:
        one.wait()
    line = lax.broadcasted_iota(jnp.int32, (rows, 1), 0)
    inside = jnp.logical_and(
        jnp.logical_or(line >= TOP, has_left), jnp.logical_or(line < TOP + points, has_right)
    )

    to_left = remote(
        u.at[:, pl.ds(TOP, 8), :], u.at[:, pl.ds(TOP + points, 8), :],
        halo_send.at[0], halo_recv.at[0], left // DEV, left % DEV,
    )
    to_right = remote(
        u.at[:, pl.ds(points, 8), :], u.at[:, pl.ds(0, 8), :],
        halo_send.at[1], halo_recv.at[1], right // DEV, right % DEV,
    )

    def slope_to(k, g):
        return remote(
            sgot.at[k], sgot.at[k], ssend.at[g], srecv.at[k], jnp.int32(g // 4), jnp.int32((g % 4) * 4)
        )

    def slope_on(k, n):
        oy, ox = OFFSETS[n]
        return remote(sgot.at[k], sgot.at[k], ssend2.at[n], srecv.at[k], s, dev_of(oy, zl, ox))

    def close_grid(k):
        drain(bgot2.at[k, pl.ds(0, 15)], brecv2.at[k])
        edge = jnp.sum(bgot2[k], axis=0) * (-kinetic * time_step / (k + 1).astype(F32))
        u[0, TOP : TOP + 1, :] += edge[1:2]
        u[1, TOP : TOP + 1, :] -= edge[0:1]
        acc[0, 0:1, :] += edge[1:2]
        acc[1, 0:1, :] -= edge[0:1]

    pl.semaphore_wait(barrier, expected)

    @pl.loop(0, TERMS)
    def _(k):
        factor = time_step / (k + 1).astype(F32)

        for n, (oy, ox) in enumerate(OFFSETS):
            ty, tx = (y + oy) % 4, (x + ox) % 4
            remote(
                stage1.at[ty * 2 + tx // 2], got1.at[k, plane], send1, recv1.at[k], s, dev_of(ty, zl, tx)
            ).start()

        @pl.when(jnp.logical_not(is_plane_root))
        def _():
            remote(bst, bgot.at[k, plane], bsend, brecv.at[k], s, dev_of(0, zl, 0)).start()

        @pl.when(is_root)
        def _():
            @pl.when(k > 0)
            def _():
                close_grid(k - 1)
                stage_slope(k)

            for g in range(1, 16):
                slope_to(k, g).start()

        @pl.when(k == 0)
        def _():
            @pl.when(has_left)
            def _():
                to_left.start()

            @pl.when(has_right)
            def _():
                to_right.start()

        got1[k, plane] = stage1[y * 2 + x // 2]

        @pl.when(is_plane_root)
        def _():
            bgot[k, 0] = bst[...]

        drain(got1.at[k, pl.ds(0, 15)], recv1.at[k])

        sums = got1[k, 0, 1:5].astype(F32)
        for p in range(1, 16):
            sums += got1[k, p, 1:5].astype(F32)
        sums = sums.astype(BF16)
        pairs = [got1[k, 2 * q, 0] + got1[k, 2 * q + 1, 0] for q in range(8)]
        for z_ in range(4):
            for q in range(8):
                stage2[z_, q] = pairs[q]
            stage2[z_, 8] = sums[z_]
            stage4[z_] = sums[z_]
        for q in range(8):
            stage3[q] = pairs[q][0:2]

        @pl.when(has_below)
        def _():
            for z_ in range(4):
                remote(stage3, above.at[k, zl], send3, recv3.at[k], s - 1, dev_of(y, z_, x)).start()

        @pl.when(has_above)
        def _():
            for z_ in range(4):
                remote(stage4.at[z_], below.at[k, zl], send4, recv4.at[k], s + 1, dev_of(y, z_, x)).start()

        for oz in (2, 1, 3):
            tz = (zl + oz) % 4
            remote(stage2.at[tz], own.at[k, zl], send2, recv2.at[k], s, dev_of(y, tz, x)).start()
        own[k, zl] = stage2[zl]

        @pl.when(is_plane_root)
        def _():
            drain(bgot.at[k, pl.ds(0, 15)], brecv.at[k])
            total = jnp.sum(bgot[k], axis=0)

            @pl.when(is_root)
            def _():
                bgot2[k, 0] = total

            @pl.when(jnp.logical_not(is_root))
            def _():
                bst2[...] = total
                remote(bst2, bgot2.at[k, group], bsend2, brecv2.at[k], jnp.int32(0), jnp.int32(0)).start()
                drain(sgot.at[k], srecv.at[k])

            for n in range(15):
                slope_on(k, n).start()

        @pl.when(k == 0)
        def _():
            @pl.when(has_left)
            def _():
                to_right.wait_recv()
                to_left.wait_send()

            @pl.when(has_right)
            def _():
                to_left.wait_recv()
                to_right.wait_send()

        images = []
        levels = env[...].reshape(1, channels)
        for i in range(2):
            value = u[i]
            mixed = jnp.dot(value.astype(BF16), lasv[...], preferred_element_type=F32)
            curve = pltpu.roll(value, 1, 0) - 2.0 * value + pltpu.roll(value, rows - 1, 0)
            image = -kinetic * curve + levels * value + laser_scale * mixed
            images.append(jnp.where(inside, image, 0.0))
        new0 = factor * images[1]
        new1 = -factor * images[0]
        u[0] = new0
        u[1] = new1
        acc[0] += new0[TOP : TOP + points]
        acc[1] += new1[TOP : TOP + points]

        @pl.when(jnp.logical_and(k == TERMS - 1, jnp.logical_not(is_root)))
        def _():
            for i in range(2):
                outer_out[i] = jnp.transpose(acc[i])

        drain(own.at[k, pl.ds(0, 3)], recv2.at[k])

        @pl.when(has_above)
        def _():
            drain(above.at[k], recv3.at[k])

        @pl.when(has_below)
        def _():
            drain(below.at[k], recv4.at[k])

        order = [(y_, z_, xh) for y_ in range(4) for z_ in range(4) for xh in range(2)]
        mine = jnp.concatenate([own[k, z_, y_ * 2 + xh] for y_, z_, xh in order], axis=1)
        upper = jnp.concatenate([above[k, z_, y_ * 2 + xh] for y_, z_, xh in order], axis=1)

        def times(vectors, matrix):
            return lax.dot_general(vectors, matrix, NT, preferred_element_type=F32)

        diag0 = times(mine, mats[0])[0:2]
        diag1 = times(mine, mats[1])[2:4]
        forward0 = times(mine, dips[0])[2:4]
        forward1 = jnp.where(has_above, times(upper, dips[1]), 0.0)

        def half_of(tile):
            return jnp.where(parity == 0, tile[:, 0:64], tile[:, 64:128])

        lower0 = below[k, 0].astype(F32)
        lower1 = own[k, 0, 8].astype(F32)
        for z_ in range(1, 4):
            lower0 += below[k, z_].astype(F32)
            lower1 += own[k, z_, 8].astype(F32)
        lower0 = jnp.where(has_below, half_of(lower0)[2:4], 0.0)
        lower1 = half_of(lower1)[0:2]
        image0 = block_scale * diag0 + dipole_scale * (forward0 + lower0)
        image1 = block_scale * diag1 + dipole_scale * (forward1 + lower1)

        @pl.when(jnp.logical_not(is_plane_root))
        def _():
            drain(sgot.at[k], srecv.at[k])

        slope = sgot[k].astype(F32)
        masked = jnp.concatenate([owned0 * slope, owned1 * slope], axis=0).astype(BF16)
        bloch = lax.dot_general(masked, ampv[...], NT, preferred_element_type=F32)
        image0 = jnp.where(live0, image0 + bloch[0:2], 0.0)
        image1 = jnp.where(live1, image1 + bloch[2:4], 0.0)
        fresh = factor * jnp.concatenate([image0[1:2], -image0[0:1], image1[1:2], -image1[0:1]], axis=0)
        wsum[...] += fresh

        drain(got1.at[k, pl.ds(0, 15)], send1)
        drain(own.at[k, pl.ds(0, 3)], send2)

        @pl.when(has_below)
        def _():
            drain(above.at[k], send3)

        @pl.when(has_above)
        def _():
            drain(below.at[k], send4)

        @pl.when(jnp.logical_not(is_plane_root))
        def _():
            drain(bst, bsend)

        @pl.when(k < TERMS - 1)
        def _():
            prepare(fresh)

        @pl.when(is_plane_root)
        def _():
            for n in range(15):
                slope_on(k, n).wait_send()

        @pl.when(is_root)
        def _():
            for g in range(1, 16):
                slope_to(k, g).wait_send()

        @pl.when(hears_root)
        def _():
            drain(bst2, bsend2)

    inner_out[0] = wsum[0:2]
    inner_out[1] = wsum[2:4]

    @pl.when(is_root)
    def _():
        close_grid(jnp.int32(TERMS - 1))
        for i in range(2):
            outer_out[i] = jnp.transpose(acc[i])


def deliver(inner_v, outer_v, inner_out, outer_out, sems):
    copies = [
        pltpu.make_async_copy(outer_v, outer_out, sems.at[0]),
        pltpu.make_async_copy(inner_v, inner_out, sems.at[1]),
    ]
    for one in copies:
        one.start()
    for one in copies:
        one.wait()


def on_device(inner, sizes, ham, dip, amps, chan, outer, energy, laser):
    blocks, parts, own_rows = inner.shape
    states = ham.shape[2]
    channels, points = outer.shape[1], outer.shape[2]
    rows = points + 16
    dma = pltpu.SemaphoreType.DMA
    anywhere = pl.BlockSpec(memory_space=pl.ANY)
    results = pl.pallas_call(
        kernel,
        out_shape=(
            pltpu.VMEM(inner.shape, F32),
            pltpu.VMEM(outer.shape, F32),
        ),
        in_specs=[anywhere] * 9,
        out_specs=(pl.BlockSpec(memory_space=pltpu.VMEM), pl.BlockSpec(memory_space=pltpu.VMEM)),
        scratch_shapes=[
            pltpu.SMEM(sizes.shape, jnp.int32),
            pltpu.VMEM(inner.shape, F32),
            pltpu.VMEM(ham.shape, BF16),
            pltpu.VMEM(dip.shape, BF16),
            pltpu.VMEM((own_rows, channels), BF16),
            pltpu.VMEM((1, channels), jnp.int32),
            pltpu.VMEM(outer.shape, F32),
            pltpu.VMEM((channels,), F32),
            pltpu.VMEM(laser.shape, BF16),
            pltpu.VMEM((2, rows, channels), F32),
            pltpu.VMEM((2, points, channels), F32),
            pltpu.VMEM((4, own_rows), F32),
            pltpu.VMEM((8, 5, 4, 128), BF16),
            pltpu.VMEM((TERMS, 16, 5, 4, 128), BF16),
            pltpu.VMEM((4, 9, 4, 128), BF16),
            pltpu.VMEM((TERMS, 4, 9, 4, 128), BF16),
            pltpu.VMEM((8, 2, 128), BF16),
            pltpu.VMEM((TERMS, 4, 8, 2, 128), BF16),
            pltpu.VMEM((4, 4, 128), BF16),
            pltpu.VMEM((TERMS, 4, 4, 128), BF16),
            pltpu.VMEM((2, channels), F32),
            pltpu.VMEM((TERMS, 16, 2, channels), F32),
            pltpu.VMEM((2, channels), F32),
            pltpu.VMEM((TERMS, 16, 2, channels), F32),
            pltpu.VMEM((TERMS, 2, channels), BF16),
            dma((9,)), dma((2,)), dma((2,)),
            dma, dma((TERMS,)), dma, dma((TERMS,)), dma, dma((TERMS,)), dma, dma((TERMS,)),
            dma, dma((TERMS,)), dma, dma((TERMS,)), dma((16,)), dma((TERMS,)), dma((15,)),
        ],
        compiler_params=pltpu.CompilerParams(
            collective_id=0, has_side_effects=True, vmem_limit_bytes=60 * 1024 * 1024
        ),
    )(
        sizes, inner, ham, dip, amps.T, chan.reshape(1, channels), outer, energy, laser,
    )
    return pl.pallas_call(
        deliver,
        out_shape=(
            jax.ShapeDtypeStruct(inner.shape, F32),
            jax.ShapeDtypeStruct(outer.shape, F32),
        ),
        in_specs=[pl.BlockSpec(memory_space=pltpu.VMEM)] * 2,
        out_specs=(anywhere, anywhere),
        scratch_shapes=[dma((2,))],
        compiler_params=pltpu.CompilerParams(vmem_limit_bytes=1024 * 1024),
    )(*results)


def solution(mesh):
    placed = (
        P("sym", None, "dev"),
        P(),
        P("sym", "dev", None),
        P("sym", "dev", None),
        P(None, "dev"),
        P(),
        P(None, None, ("sym", "dev")),
        P(),
        P(),
    )
    return jax.shard_map(
        on_device,
        mesh=mesh,
        in_specs=placed,
        out_specs=(P("sym", None, "dev"), P(None, None, ("sym", "dev"))),
        check_vma=False,
    )
```

time: 63.4 us -> 54.2 us (0.85)
  local copies, waits for them, and re-layouts: 4.6 us -> 0 us
  Pallas kernels: 58 us -> 53.5 us
    pallas_call x1 -> x2, Pallas kernels: 58 us -> 53.5 us  [the longest x1 52.6 us: on_device(): pl.pallas_call(kernel, out_shape=(pltpu.VMEM(inner.shape, F32), pltpu.VME...]
    unnamed x2 -> x0, local copies, waits for them, and re-layouts: 3.33 us -> none
    reshape x1 -> x0, local copies, waits for them, and re-layouts: 1.27 us -> none  [on_device(): energy.reshape(1, channels)]
where the time goes in v2:
time: 54.2 us
  Pallas kernels  53.5 us (99%)
  between operations  0.64 us (1%)
    pallas_call x1, Pallas kernels, on_device(): pl.pallas_call(kernel, out_shape=(pltpu.VMEM(inner.shape, F32), pltpu.VME...  52.6 us

profile of v2, /device:TPU:1, one launch (start us, length us, event | category | flops | bytes accessed | tf_op | source)
XLA Modules:
  0.0 54.2 jit_solution(13319848297047389615)
XLA Ops:
  0.6 52.6 %shard_map.104 = (f32[2,2,64]{2,1,0:T(2,128)S(1)}, f32[2,800,128]{2,1,0:T(8,128)S(1)}) custom-call(s32[8]{0:T(128)} %sizes_in.1, f32[2,2,64]{2,1,0:T(2,128)} %inner.1, bf16[2,64,4096]{2,1,0:T(8,128)(2,1)} %ham.1, bf16[2,64,4096]{2,1,0:T(8,128)(2,1)} %dip.1, bf16[64,800]{1,0:T(8,128)(2,1)} %bitcast.2, s32[1,800]{1,0:T(1,128)} %bitcast.3, ...), custom_call_target="tpu_custom_call" | custom-call | tf_op jit(solution)/shard_map/pallas_call | solution.py:460
  53.2 0.9 %shard_map.105 = (f32[2,2,64]{2,1,0:T(2,128)}, f32[2,800,128]{2,1,0:T(8,128)}) custom-call(f32[2,2,64]{2,1,0:T(2,128)S(1)} %get-tuple-element.4.inner_v, f32[2,800,128]{2,1,0:T(8,128)S(1)} %get-tuple-element.5.outer_v), custom_call_target="tpu_custom_call" | custom-call | tf_op jit(solution)/shard_map/pallas_call | solution.py:504

commit v3 on v2

--- a/solution.py
+++ b/solution.py
@@ -48,8 +48,10 @@
     inner_out, outer_out,
     sizes, inn, mats, dips, ampv, chv, out_raw, env, lasv, u, acc, wsum,
     stage1, got1, stage2, own, stage3, above, stage4, below,
+    staged, first2, got, above_d, below_d, lows, highs, lower_h, upper_h,
     bst, bgot, bst2, bgot2, sgot,
     load, halo_send, halo_recv, send1, recv1, send2, recv2, send3, recv3, send4, recv4,
+    sendd, recvd, sendx, recvx, sendh, recvh,
     bsend, brecv, bsend2, brecv2, ssend, srecv, ssend2,
 ):
     s = lax.axis_index("sym")
@@ -137,7 +139,7 @@
     zero2 = jnp.zeros((2, 64), BF16)
     zero4 = jnp.zeros((4, 64), BF16)
 
-    def prepare(state):
+    def products(state):
         half = state.astype(BF16)
         spread = jnp.concatenate(
             [jnp.concatenate([half[0:2], zero2], axis=1), jnp.concatenate([zero2, half[2:4]], axis=1)], axis=0
@@ -147,14 +149,25 @@
         even = jnp.concatenate([half, zero4], axis=1)
         odd = jnp.concatenate([zero4, half], axis=1)
         chunk = jnp.where(parity == 0, even, odd)
+        per_block = jnp.dot(half, ampv[...], preferred_element_type=F32)
+        bst[...] = owned0 * per_block[0:2] + owned1 * per_block[2:4]
+        return chunk, part
+
+    def prepare_plane(state):
+        chunk, part = products(state)
         for y_ in range(4):
             for xh in range(2):
                 stage1[y_ * 2 + xh, 0] = chunk
                 for z_ in range(4):
                     tile = (y_ * 4 + z_) * 2 + xh
                     stage1[y_ * 2 + xh, 1 + z_] = part[:, tile * 128 : (tile + 1) * 128]
-        per_block = jnp.dot(half, ampv[...], preferred_element_type=F32)
-        bst[...] = owned0 * per_block[0:2] + owned1 * per_block[2:4]
+
+    def prepare_direct(state):
+        chunk, part = products(state)
+        first2[...] = chunk[0:2]
+        for tile in range(32):
+            staged[tile, 0] = chunk
+            staged[tile, 1] = part[:, tile * 128 : (tile + 1) * 128]
 
     first = jnp.concatenate(
         [jnp.where(live0, inn[0], 0.0), jnp.where(live1, inn[1], 0.0)], axis=0
@@ -164,7 +177,7 @@
     loads[4].wait()
     owned0 = (chv[...] == 2 * s).astype(F32)
     owned1 = (chv[...] == 2 * s + 1).astype(F32)
-    prepare(first)
+    prepare_plane(first)
 
     loads[5].wait()
     blank = jnp.zeros((2, TOP, channels), F32)
@@ -219,116 +232,51 @@
         oy, ox = OFFSETS[n]
         return remote(sgot.at[k], sgot.at[k], ssend2.at[n], srecv.at[k], s, dev_of(oy, zl, ox))
 
+    def factor_of(k):
+        return time_step / (k + 1) if isinstance(k, int) else time_step / (k + 1).astype(F32)
+
     def close_grid(k):
         drain(bgot2.at[k, pl.ds(0, 15)], brecv2.at[k])
-        edge = jnp.sum(bgot2[k], axis=0) * (-kinetic * time_step / (k + 1).astype(F32))
+        edge = jnp.sum(bgot2[k], axis=0) * (-kinetic * factor_of(k))
         u[0, TOP : TOP + 1, :] += edge[1:2]
         u[1, TOP : TOP + 1, :] -= edge[0:1]
         acc[0, 0:1, :] += edge[1:2]
         acc[1, 0:1, :] -= edge[0:1]
 
-    pl.semaphore_wait(barrier, expected)
-
-    @pl.loop(0, TERMS)
-    def _(k):
-        factor = time_step / (k + 1).astype(F32)
-
-        for n, (oy, ox) in enumerate(OFFSETS):
-            ty, tx = (y + oy) % 4, (x + ox) % 4
-            remote(
-                stage1.at[ty * 2 + tx // 2], got1.at[k, plane], send1, recv1.at[k], s, dev_of(ty, zl, tx)
-            ).start()
+    def send_boundary(k):
+        @pl.when(is_plane_root)
+        def _():
+            bgot[k, 0] = bst[...]
 
         @pl.when(jnp.logical_not(is_plane_root))
         def _():
             remote(bst, bgot.at[k, plane], bsend, brecv.at[k], s, dev_of(0, zl, 0)).start()
 
+    def send_slope(k):
+        for g in range(1, 16):
+            slope_to(k, g).start()
+
+    def relay(k):
+        @pl.when(hears_root)
+        def _():
+            drain(sgot.at[k], srecv.at[k])
+
+        for n in range(15):
+            slope_on(k, n).start()
+        drain(bgot.at[k, pl.ds(0, 15)], brecv.at[k])
+        total = jnp.sum(bgot[k], axis=0)
+
         @pl.when(is_root)
         def _():
-            @pl.when(k > 0)
-            def _():
-                close_grid(k - 1)
-                stage_slope(k)
-
-            for g in range(1, 16):
-                slope_to(k, g).start()
-
-        @pl.when(k == 0)
-        def _():
-            @pl.when(has_left)
-            def _():
-                to_left.start()
-
-            @pl.when(has_right)
-            def _():
-                to_right.start()
-
-        got1[k, plane] = stage1[y * 2 + x // 2]
-
-        @pl.when(is_plane_root)
-        def _():
-            bgot[k, 0] = bst[...]
-
-        drain(got1.at[k, pl.ds(0, 15)], recv1.at[k])
-
-        sums = got1[k, 0, 1:5].astype(F32)
-        for p in range(1, 16):
-            sums += got1[k, p, 1:5].astype(F32)
-        sums = sums.astype(BF16)
-        pairs = [got1[k, 2 * q, 0] + got1[k, 2 * q + 1, 0] for q in range(8)]
-        for z_ in range(4):
-            for q in range(8):
-                stage2[z_, q] = pairs[q]
-            stage2[z_, 8] = sums[z_]
-            stage4[z_] = sums[z_]
-        for q in range(8):
-            stage3[q] = pairs[q][0:2]
-
-        @pl.when(has_below)
-        def _():
-            for z_ in range(4):
-                remote(stage3, above.at[k, zl], send3, recv3.at[k], s - 1, dev_of(y, z_, x)).start()
-
-        @pl.when(has_above)
-        def _():
-            for z_ in range(4):
-                remote(stage4.at[z_], below.at[k, zl], send4, recv4.at[k], s + 1, dev_of(y, z_, x)).start()
-
-        for oz in (2, 1, 3):
-            tz = (zl + oz) % 4
-            remote(stage2.at[tz], own.at[k, zl], send2, recv2.at[k], s, dev_of(y, tz, x)).start()
-        own[k, zl] = stage2[zl]
-
-        @pl.when(is_plane_root)
-        def _():
-            drain(bgot.at[k, pl.ds(0, 15)], brecv.at[k])
-            total = jnp.sum(bgot[k], axis=0)
-
-            @pl.when(is_root)
-            def _():
-                bgot2[k, 0] = total
-
-            @pl.when(jnp.logical_not(is_root))
-            def _():
-                bst2[...] = total
-                remote(bst2, bgot2.at[k, group], bsend2, brecv2.at[k], jnp.int32(0), jnp.int32(0)).start()
-                drain(sgot.at[k], srecv.at[k])
-
-            for n in range(15):
-                slope_on(k, n).start()
-
-        @pl.when(k == 0)
-        def _():
-            @pl.when(has_left)
-            def _():
-                to_right.wait_recv()
-                to_left.wait_send()
-
-            @pl.when(has_right)
-            def _():
-                to_left.wait_recv()
-                to_right.wait_send()
-
+            bgot2[k, 0] = total
+
+        @pl.when(hears_root)
+        def _():
+            bst2[...] = total
+            remote(bst2, bgot2.at[k, group], bsend2, brecv2.at[k], jnp.int32(0), jnp.int32(0)).start()
+
+    def outer_update(k):
+        factor = factor_of(k)
         images = []
         levels = env[...].reshape(1, channels)
         for i in range(2):
@@ -344,46 +292,13 @@
         acc[0] += new0[TOP : TOP + points]
         acc[1] += new1[TOP : TOP + points]
 
-        @pl.when(jnp.logical_and(k == TERMS - 1, jnp.logical_not(is_root)))
-        def _():
-            for i in range(2):
-                outer_out[i] = jnp.transpose(acc[i])
-
-        drain(own.at[k, pl.ds(0, 3)], recv2.at[k])
-
-        @pl.when(has_above)
-        def _():
-            drain(above.at[k], recv3.at[k])
-
-        @pl.when(has_below)
-        def _():
-            drain(below.at[k], recv4.at[k])
-
-        order = [(y_, z_, xh) for y_ in range(4) for z_ in range(4) for xh in range(2)]
-        mine = jnp.concatenate([own[k, z_, y_ * 2 + xh] for y_, z_, xh in order], axis=1)
-        upper = jnp.concatenate([above[k, z_, y_ * 2 + xh] for y_, z_, xh in order], axis=1)
-
-        def times(vectors, matrix):
-            return lax.dot_general(vectors, matrix, NT, preferred_element_type=F32)
-
-        diag0 = times(mine, mats[0])[0:2]
-        diag1 = times(mine, mats[1])[2:4]
-        forward0 = times(mine, dips[0])[2:4]
-        forward1 = jnp.where(has_above, times(upper, dips[1]), 0.0)
-
-        def half_of(tile):
-            return jnp.where(parity == 0, tile[:, 0:64], tile[:, 64:128])
-
-        lower0 = below[k, 0].astype(F32)
-        lower1 = own[k, 0, 8].astype(F32)
-        for z_ in range(1, 4):
-            lower0 += below[k, z_].astype(F32)
-            lower1 += own[k, z_, 8].astype(F32)
-        lower0 = jnp.where(has_below, half_of(lower0)[2:4], 0.0)
-        lower1 = half_of(lower1)[0:2]
-        image0 = block_scale * diag0 + dipole_scale * (forward0 + lower0)
-        image1 = block_scale * diag1 + dipole_scale * (forward1 + lower1)
-
+    def times(vectors, matrix):
+        return lax.dot_general(vectors, matrix, NT, preferred_element_type=F32)
+
+    def half_of(tile):
+        return jnp.where(parity == 0, tile[:, 0:64], tile[:, 64:128])
+
+    def finish(k, image0, image1):
         @pl.when(jnp.logical_not(is_plane_root))
         def _():
             drain(sgot.at[k], srecv.at[k])
@@ -393,28 +308,18 @@
         bloch = lax.dot_general(masked, ampv[...], NT, preferred_element_type=F32)
         image0 = jnp.where(live0, image0 + bloch[0:2], 0.0)
         image1 = jnp.where(live1, image1 + bloch[2:4], 0.0)
-        fresh = factor * jnp.concatenate([image0[1:2], -image0[0:1], image1[1:2], -image1[0:1]], axis=0)
+        fresh = factor_of(k) * jnp.concatenate(
+            [image0[1:2], -image0[0:1], image1[1:2], -image1[0:1]], axis=0
+        )
         wsum[...] += fresh
 
-        drain(got1.at[k, pl.ds(0, 15)], send1)
-        drain(own.at[k, pl.ds(0, 3)], send2)
-
-        @pl.when(has_below)
-        def _():
-            drain(above.at[k], send3)
-
-        @pl.when(has_above)
-        def _():
-            drain(below.at[k], send4)
-
         @pl.when(jnp.logical_not(is_plane_root))
         def _():
             drain(bst, bsend)
 
-        @pl.when(k < TERMS - 1)
-        def _():
-            prepare(fresh)
-
+        return fresh
+
+    def sent_slope(k):
         @pl.when(is_plane_root)
         def _():
             for n in range(15):
@@ -429,12 +334,241 @@
         def _():
             drain(bst2, bsend2)
 
+    pl.semaphore_wait(barrier, expected)
+
+    for n, (oy, ox) in enumerate(OFFSETS):
+        ty, tx = (y + oy) % 4, (x + ox) % 4
+        remote(
+            stage1.at[ty * 2 + tx // 2], got1.at[plane], send1, recv1, s, dev_of(ty, zl, tx)
+        ).start()
+    send_boundary(0)
+
+    @pl.when(is_root)
+    def _():
+        send_slope(0)
+
+    @pl.when(has_left)
+    def _():
+        to_left.start()
+
+    @pl.when(has_right)
+    def _():
+        to_right.start()
+
+    got1[plane] = stage1[y * 2 + x // 2]
+    drain(got1.at[pl.ds(0, 15)], recv1)
+
+    sums = got1[0, 1:5].astype(F32)
+    for p in range(1, 16):
+        sums += got1[p, 1:5].astype(F32)
+    sums = sums.astype(BF16)
+    tiles = [got1[2 * q, 0] + got1[2 * q + 1, 0] for q in range(8)]
+    for z_ in range(4):
+        for q in range(8):
+            stage2[z_, q] = tiles[q]
+        stage2[z_, 8] = sums[z_]
+        stage4[z_] = sums[z_]
+    for q in range(8):
+        stage3[q] = tiles[q][0:2]
+
+    @pl.when(has_below)
+    def _():
+        for z_ in range(4):
+            remote(stage3, above.at[zl], send3, recv3, s - 1, dev_of(y, z_, x)).start()
+
+    @pl.when(has_above)
+    def _():
+        for z_ in range(4):
+            remote(stage4.at[z_], below.at[zl], send4, recv4, s + 1, dev_of(y, z_, x)).start()
+
+    for oz in (2, 1, 3):
+        tz = (zl + oz) % 4
+        remote(stage2.at[tz], own.at[zl], send2, recv2, s, dev_of(y, tz, x)).start()
+    own[zl] = stage2[zl]
+
+    @pl.when(is_plane_root)
+    def _():
+        relay(0)
+
+    @pl.when(has_left)
+    def _():
+        to_right.wait_recv()
+        to_left.wait_send()
+
+    @pl.when(has_right)
+    def _():
+        to_left.wait_recv()
+        to_right.wait_send()
+
+    outer_update(0)
+
+    @pl.when(is_root)
+    def _():
+        close_grid(0)
+        stage_slope(1)
+        send_slope(1)
+
+    drain(own.at[pl.ds(0, 3)], recv2)
+
+    @pl.when(has_above)
+    def _():
+        drain(above, recv3)
+
+    @pl.when(has_below)
+    def _():
+        drain(below, recv4)
+
+    order = [(y_, z_, xh) for y_ in range(4) for z_ in range(4) for xh in range(2)]
+    mine = jnp.concatenate([own[z_, y_ * 2 + xh] for y_, z_, xh in order], axis=1)
+    upper = jnp.concatenate([above[z_, y_ * 2 + xh] for y_, z_, xh in order], axis=1)
+    lower0 = below[0].astype(F32)
+    lower1 = own[0, 8].astype(F32)
+    for z_ in range(1, 4):
+        lower0 += below[z_].astype(F32)
+        lower1 += own[z_, 8].astype(F32)
+    lower0 = jnp.where(has_below, half_of(lower0)[2:4], 0.0)
+    lower1 = half_of(lower1)[0:2]
+    forward1 = jnp.where(has_above, times(upper, dips[1]), 0.0)
+    image0 = block_scale * times(mine, mats[0])[0:2] + dipole_scale * (times(mine, dips[0])[2:4] + lower0)
+    image1 = block_scale * times(mine, mats[1])[2:4] + dipole_scale * (forward1 + lower1)
+    fresh = finish(0, image0, image1)
+    prepare_direct(fresh)
+    drain(got1.at[pl.ds(0, 15)], send1)
+    drain(own.at[pl.ds(0, 3)], send2)
+
+    @pl.when(has_below)
+    def _():
+        drain(above, send3)
+
+    @pl.when(has_above)
+    def _():
+        drain(below, send4)
+
+    sent_slope(0)
+    partner = s + 1 - 2 * (s % 2)
+    is_low = s % 2 == 0
+    is_high = s % 2 == 1
+
+    @pl.loop(1, TERMS)
+    def _(k):
+        send_boundary(k)
+        for level in range(4, -1, -1):
+            ring = [o for o in OFFSETS + [(0, 0)] if torus(o[0]) + torus(o[1]) == level]
+            targets = [
+                (dev_of((y + oy) % 4, (zl + oz) % 4, (x + ox) % 4), (oy, oz, ox)) for oz in (2, 1, 3, 0) for oy, ox in ring
+            ]
+
+            @pl.when(s == 1)
+            def _():
+                for to, _o in targets:
+                    remote(staged.at[to // 2, 1], below_d.at[k, d], sendx, recvx.at[k], jnp.int32(2), to).start()
+
+            @pl.when(s == 2)
+            def _():
+                for to, _o in targets:
+                    remote(first2, above_d.at[k, d], sendx, recvx.at[k], jnp.int32(1), to).start()
+
+            for to, offset in targets:
+                if offset != (0, 0, 0):
+                    remote(staged.at[to // 2], got.at[k, d], sendd, recvd.at[k], s, to).start()
+
+        got[k, d] = staged[d // 2]
+
+        @pl.when(is_plane_root)
+        def _():
+            relay(k)
+
+        outer_update(k)
+
+        @pl.when(jnp.logical_and(k == TERMS - 1, jnp.logical_not(is_root)))
+        def _():
+            for i in range(2):
+                outer_out[i] = jnp.transpose(acc[i])
+
+        @pl.when(jnp.logical_and(is_root, k < TERMS - 1))
+        def _():
+            close_grid(k)
+            stage_slope(k + 1)
+            send_slope(k + 1)
+
+        drain(got.at[k, pl.ds(0, 63)], recvd.at[k])
+        sums = got[k, 0, 1].astype(F32)
+        for p in range(1, 64):
+            sums += got[k, p, 1].astype(F32)
+        mine = jnp.concatenate([got[k, 2 * q, 0] + got[k, 2 * q + 1, 0] for q in range(32)], axis=1)
+
+        give_low = remote(lows, lower_h.at[k], sendh, recvh.at[k], partner, d)
+        give_high = remote(highs, upper_h.at[k], sendh, recvh.at[k], partner, d)
+
+        @pl.when(is_low)
+        def _():
+            lows[...] = sums[2:4]
+            give_low.start()
+
+        @pl.when(is_high)
+        def _():
+            highs[...] = mine[0:2]
+            give_high.start()
+
+        image0 = block_scale * times(mine, mats[0])[0:2] + dipole_scale * times(mine, dips[0])[2:4]
+        image1 = block_scale * times(mine, mats[1])[2:4] + dipole_scale * half_of(sums)[0:2]
+
+        @pl.when(s == 1)
+        def _():
+            drain(above_d.at[k], recvx.at[k])
+            for q in range(32):
+                upper_h[k, :, q * 128 : (q + 1) * 128] = above_d[k, 2 * q] + above_d[k, 2 * q + 1]
+
+        @pl.when(s == 2)
+        def _():
+            drain(below_d.at[k], recvx.at[k])
+            total = below_d[k, 0].astype(F32)
+            for p in range(1, 64):
+                total += below_d[k, p].astype(F32)
+            lower_h[k] = total[2:4]
+
+        @pl.when(is_low)
+        def _():
+            drain(upper_h.at[k], recvh.at[k])
+
+        @pl.when(is_high)
+        def _():
+            drain(lower_h.at[k], recvh.at[k])
+
+        image0 += jnp.where(has_below, dipole_scale * half_of(lower_h[k]), 0.0)
+        image1 += jnp.where(has_above, dipole_scale * times(upper_h[k], dips[1]), 0.0)
+        fresh = finish(k, image0, image1)
+
+        drain(got.at[k, pl.ds(0, 63)], sendd)
+
+        @pl.when(s == 1)
+        def _():
+            drain(below_d.at[k], sendx)
+
+        @pl.when(s == 2)
+        def _():
+            drain(above_d.at[k], sendx)
+
+        @pl.when(k < TERMS - 1)
+        def _():
+            prepare_direct(fresh)
+
+        @pl.when(is_low)
+        def _():
+            drain(lower_h.at[k], sendh)
+
+        @pl.when(is_high)
+        def _():
+            drain(upper_h.at[k], sendh)
+
+        sent_slope(k)
+
     inner_out[0] = wsum[0:2]
     inner_out[1] = wsum[2:4]
 
     @pl.when(is_root)
     def _():
-        close_grid(jnp.int32(TERMS - 1))
+        close_grid(TERMS - 1)
         for i in range(2):
             outer_out[i] = jnp.transpose(acc[i])
 
@@ -479,20 +613,30 @@
             pltpu.VMEM((2, points, channels), F32),
             pltpu.VMEM((4, own_rows), F32),
             pltpu.VMEM((8, 5, 4, 128), BF16),
-            pltpu.VMEM((TERMS, 16, 5, 4, 128), BF16),
+            pltpu.VMEM((16, 5, 4, 128), BF16),
             pltpu.VMEM((4, 9, 4, 128), BF16),
-            pltpu.VMEM((TERMS, 4, 9, 4, 128), BF16),
+            pltpu.VMEM((4, 9, 4, 128), BF16),
             pltpu.VMEM((8, 2, 128), BF16),
-            pltpu.VMEM((TERMS, 4, 8, 2, 128), BF16),
+            pltpu.VMEM((4, 8, 2, 128), BF16),
             pltpu.VMEM((4, 4, 128), BF16),
-            pltpu.VMEM((TERMS, 4, 4, 128), BF16),
+            pltpu.VMEM((4, 4, 128), BF16),
+            pltpu.VMEM((32, 2, 4, 128), BF16),
+            pltpu.VMEM((2, 128), BF16),
+            pltpu.VMEM((TERMS, 64, 2, 4, 128), BF16),
+            pltpu.VMEM((TERMS, 64, 2, 128), BF16),
+            pltpu.VMEM((TERMS, 64, 4, 128), BF16),
+            pltpu.VMEM((2, 128), F32),
+            pltpu.VMEM((2, states), BF16),
+            pltpu.VMEM((TERMS, 2, 128), F32),
+            pltpu.VMEM((TERMS, 2, states), BF16),
             pltpu.VMEM((2, channels), F32),
             pltpu.VMEM((TERMS, 16, 2, channels), F32),
             pltpu.VMEM((2, channels), F32),
             pltpu.VMEM((TERMS, 16, 2, channels), F32),
             pltpu.VMEM((TERMS, 2, channels), BF16),
             dma((9,)), dma((2,)), dma((2,)),
-            dma, dma((TERMS,)), dma, dma((TERMS,)), dma, dma((TERMS,)), dma, dma((TERMS,)),
+            dma, dma, dma, dma, dma, dma, dma, dma,
+            dma, dma((TERMS,)), dma, dma((TERMS,)), dma, dma((TERMS,)),
             dma, dma((TERMS,)), dma, dma((TERMS,)), dma((16,)), dma((TERMS,)), dma((15,)),
         ],
         compiler_params=pltpu.CompilerParams(

time: 54.2 us -> 52.3 us (0.965)
  Pallas kernels: 53.5 us -> 51.6 us
    pallas_call x1, Pallas kernels: 52.6 us -> 50.7 us  [on_device(): pl.pallas_call(kernel, out_shape=(pltpu.VMEM(inner.shape, F32), pltpu.VME...]
where the time goes in v3:
time: 52.3 us; the launch traced here: 52.2 us
  Pallas kernels  51.6 us (99%)
  between operations  0.64 us (1%)
    pallas_call x1, Pallas kernels, on_device(): pl.pallas_call(kernel, out_shape=(pltpu.VMEM(inner.shape, F32), pltpu.VME...  50.7 us

profile of v3, /device:TPU:1, one launch (start us, length us, event | category | flops | bytes accessed | tf_op | source)
XLA Modules:
  0.0 52.2 jit_solution(7506290135211039197)
XLA Ops:
  0.6 50.7 %shard_map.104 = (f32[2,2,64]{2,1,0:T(2,128)S(1)}, f32[2,800,128]{2,1,0:T(8,128)S(1)}) custom-call(s32[8]{0:T(128)} %sizes_in.1, f32[2,2,64]{2,1,0:T(2,128)} %inner.1, bf16[2,64,4096]{2,1,0:T(8,128)(2,1)} %ham.1, bf16[2,64,4096]{2,1,0:T(8,128)(2,1)} %dip.1, bf16[64,800]{1,0:T(8,128)(2,1)} %bitcast.2, s32[1,800]{1,0:T(1,128)} %bitcast.3, ...), custom_call_target="tpu_custom_call" | custom-call | tf_op jit(solution)/shard_map/pallas_call | solution.py:594
  51.3 0.9 %shard_map.105 = (f32[2,2,64]{2,1,0:T(2,128)}, f32[2,800,128]{2,1,0:T(8,128)}) custom-call(f32[2,2,64]{2,1,0:T(2,128)S(1)} %get-tuple-element.4.inner_v, f32[2,800,128]{2,1,0:T(8,128)S(1)} %get-tuple-element.5.outer_v), custom_call_target="tpu_custom_call" | custom-call | tf_op jit(solution)/shard_map/pallas_call | solution.py:648

commit v4 on v3

--- a/solution.py
+++ b/solution.py
@@ -149,9 +149,11 @@
         even = jnp.concatenate([half, zero4], axis=1)
         odd = jnp.concatenate([zero4, half], axis=1)
         chunk = jnp.where(parity == 0, even, odd)
-        per_block = jnp.dot(half, ampv[...], preferred_element_type=F32)
+        return chunk, part
+
+    def stage_boundary(state):
+        per_block = jnp.dot(state.astype(BF16), ampv[...], preferred_element_type=F32)
         bst[...] = owned0 * per_block[0:2] + owned1 * per_block[2:4]
-        return chunk, part
 
     def prepare_plane(state):
         chunk, part = products(state)
@@ -178,6 +180,7 @@
     owned0 = (chv[...] == 2 * s).astype(F32)
     owned1 = (chv[...] == 2 * s + 1).astype(F32)
     prepare_plane(first)
+    stage_boundary(first)
 
     loads[5].wait()
     blank = jnp.zeros((2, TOP, channels), F32)
@@ -298,16 +301,23 @@
     def half_of(tile):
         return jnp.where(parity == 0, tile[:, 0:64], tile[:, 64:128])
 
-    def finish(k, image0, image1):
+    def slope_term(k):
         @pl.when(jnp.logical_not(is_plane_root))
         def _():
             drain(sgot.at[k], srecv.at[k])
 
         slope = sgot[k].astype(F32)
         masked = jnp.concatenate([owned0 * slope, owned1 * slope], axis=0).astype(BF16)
-        bloch = lax.dot_general(masked, ampv[...], NT, preferred_element_type=F32)
-        image0 = jnp.where(live0, image0 + bloch[0:2], 0.0)
-        image1 = jnp.where(live1, image1 + bloch[2:4], 0.0)
+        return lax.dot_general(masked, ampv[...], NT, preferred_element_type=F32)
+
+    def next_slope(k):
+        close_grid(k)
+        stage_slope(k + 1)
+        send_slope(k + 1)
+
+    def finish(k, image0, image1):
+        image0 = jnp.where(live0, image0, 0.0)
+        image1 = jnp.where(live1, image1, 0.0)
         fresh = factor_of(k) * jnp.concatenate(
             [image0[1:2], -image0[0:1], image1[1:2], -image1[0:1]], axis=0
         )
@@ -317,6 +327,14 @@
         def _():
             drain(bst, bsend)
 
+        def ahead():
+            stage_boundary(fresh)
+            send_boundary(k + 1)
+
+        if isinstance(k, int):
+            ahead()
+        else:
+            pl.when(k < TERMS - 1)(ahead)
         return fresh
 
     def sent_slope(k):
@@ -336,12 +354,12 @@
 
     pl.semaphore_wait(barrier, expected)
 
+    send_boundary(0)
     for n, (oy, ox) in enumerate(OFFSETS):
         ty, tx = (y + oy) % 4, (x + ox) % 4
         remote(
             stage1.at[ty * 2 + tx // 2], got1.at[plane], send1, recv1, s, dev_of(ty, zl, tx)
         ).start()
-    send_boundary(0)
 
     @pl.when(is_root)
     def _():
@@ -401,12 +419,6 @@
         to_right.wait_send()
 
     outer_update(0)
-
-    @pl.when(is_root)
-    def _():
-        close_grid(0)
-        stage_slope(1)
-        send_slope(1)
 
     drain(own.at[pl.ds(0, 3)], recv2)
 
@@ -431,7 +443,13 @@
     forward1 = jnp.where(has_above, times(upper, dips[1]), 0.0)
     image0 = block_scale * times(mine, mats[0])[0:2] + dipole_scale * (times(mine, dips[0])[2:4] + lower0)
     image1 = block_scale * times(mine, mats[1])[2:4] + dipole_scale * (forward1 + lower1)
-    fresh = finish(0, image0, image1)
+    bloch = slope_term(0)
+    fresh = finish(0, image0 + bloch[0:2], image1 + bloch[2:4])
+
+    @pl.when(is_root)
+    def _():
+        next_slope(0)
+
     prepare_direct(fresh)
     drain(got1.at[pl.ds(0, 15)], send1)
     drain(own.at[pl.ds(0, 3)], send2)
@@ -451,7 +469,6 @@
 
     @pl.loop(1, TERMS)
     def _(k):
-        send_boundary(k)
         for level in range(4, -1, -1):
             ring = [o for o in OFFSETS + [(0, 0)] if torus(o[0]) + torus(o[1]) == level]
             targets = [
@@ -485,33 +502,35 @@
             for i in range(2):
                 outer_out[i] = jnp.transpose(acc[i])
 
-        @pl.when(jnp.logical_and(is_root, k < TERMS - 1))
-        def _():
-            close_grid(k)
-            stage_slope(k + 1)
-            send_slope(k + 1)
-
         drain(got.at[k, pl.ds(0, 63)], recvd.at[k])
+        give_low = remote(lows, lower_h.at[k], sendh, recvh.at[k], partner, d)
+        give_high = remote(highs, upper_h.at[k], sendh, recvh.at[k], partner, d)
+
+        @pl.when(is_high)
+        def _():
+            for q in range(32):
+                highs[:, q * 128 : (q + 1) * 128] = got[k, 2 * q, 0, 0:2] + got[k, 2 * q + 1, 0, 0:2]
+            give_high.start()
+
         sums = got[k, 0, 1].astype(F32)
         for p in range(1, 64):
             sums += got[k, p, 1].astype(F32)
-        mine = jnp.concatenate([got[k, 2 * q, 0] + got[k, 2 * q + 1, 0] for q in range(32)], axis=1)
-
-        give_low = remote(lows, lower_h.at[k], sendh, recvh.at[k], partner, d)
-        give_high = remote(highs, upper_h.at[k], sendh, recvh.at[k], partner, d)
 
         @pl.when(is_low)
         def _():
             lows[...] = sums[2:4]
             give_low.start()
 
-        @pl.when(is_high)
-        def _():
-            highs[...] = mine[0:2]
-            give_high.start()
-
+        mine = jnp.concatenate([got[k, 2 * q, 0] + got[k, 2 * q + 1, 0] for q in range(32)], axis=1)
         image0 = block_scale * times(mine, mats[0])[0:2] + dipole_scale * times(mine, dips[0])[2:4]
         image1 = block_scale * times(mine, mats[1])[2:4] + dipole_scale * half_of(sums)[0:2]
+        bloch = slope_term(k)
+        image0 += bloch[0:2]
+        image1 += bloch[2:4]
+
+        @pl.when(jnp.logical_and(is_root, k < TERMS - 1))
+        def _():
+            next_slope(k)
 
         @pl.when(s == 1)
         def _():

time: 52.3 us -> 50.6 us (0.967)
  Pallas kernels: 51.6 us -> 49.9 us
    pallas_call x1, Pallas kernels: 50.7 us -> 49 us  [on_device(): pl.pallas_call(kernel, out_shape=(pltpu.VMEM(inner.shape, F32), pltpu.VME...]
where the time goes in v4:
time: 50.6 us; the launch traced here: 50.5 us
  Pallas kernels  49.9 us (99%)
  between operations  0.64 us (1%)
    pallas_call x1, Pallas kernels, on_device(): pl.pallas_call(kernel, out_shape=(pltpu.VMEM(inner.shape, F32), pltpu.VME...  49 us

profile of v4, /device:TPU:1, one launch (start us, length us, event | category | flops | bytes accessed | tf_op | source)
XLA Modules:
  0.0 50.5 jit_solution(6566030481303043709)
XLA Ops:
  0.6 49.0 %shard_map.104 = (f32[2,2,64]{2,1,0:T(2,128)S(1)}, f32[2,800,128]{2,1,0:T(8,128)S(1)}) custom-call(s32[8]{0:T(128)} %sizes_in.1, f32[2,2,64]{2,1,0:T(2,128)} %inner.1, bf16[2,64,4096]{2,1,0:T(8,128)(2,1)} %ham.1, bf16[2,64,4096]{2,1,0:T(8,128)(2,1)} %dip.1, bf16[64,800]{1,0:T(8,128)(2,1)} %bitcast.2, s32[1,800]{1,0:T(1,128)} %bitcast.3, ...), custom_call_target="tpu_custom_call" | custom-call | tf_op jit(solution)/shard_map/pallas_call | solution.py:613
  49.6 0.9 %shard_map.105 = (f32[2,2,64]{2,1,0:T(2,128)}, f32[2,800,128]{2,1,0:T(8,128)}) custom-call(f32[2,2,64]{2,1,0:T(2,128)S(1)} %get-tuple-element.4.inner_v, f32[2,800,128]{2,1,0:T(8,128)S(1)} %get-tuple-element.5.outer_v), custom_call_target="tpu_custom_call" | custom-call | tf_op jit(solution)/shard_map/pallas_call | solution.py:667

commit v5 on v4

--- a/solution.py
+++ b/solution.py
@@ -70,6 +70,14 @@
     def dev_of(y_, z_, x_):
         return (y_ * 4 + z_) * 4 + x_
 
+    pairs = (
+        (sizes_in, sizes), (inner, inn), (dip, dips), (amps, ampv), (chan, chv),
+        (outer, out_raw), (energy, env), (laser, lasv), (ham, mats),
+    )
+    loads = [pltpu.make_async_copy(src, dst, load.at[n]) for n, (src, dst) in enumerate(pairs)]
+    for one in loads[:3]:
+        one.start()
+
     barrier = pltpu.get_barrier_semaphore()
 
     def greet(sym, dev):
@@ -122,12 +130,7 @@
 
     expected += has_left.astype(jnp.int32) + has_right.astype(jnp.int32)
 
-    pairs = (
-        (sizes_in, sizes), (inner, inn), (dip, dips), (amps, ampv), (chan, chv),
-        (outer, out_raw), (energy, env), (laser, lasv), (ham, mats),
-    )
-    loads = [pltpu.make_async_copy(src, dst, load.at[n]) for n, (src, dst) in enumerate(pairs)]
-    for one in loads:
+    for one in loads[3:]:
         one.start()
 
     for one in loads[0:3]:
@@ -182,22 +185,6 @@
     prepare_plane(first)
     stage_boundary(first)
 
-    loads[5].wait()
-    blank = jnp.zeros((2, TOP, channels), F32)
-
-    @pl.when(is_root)
-    def _():
-        u[:, 0:TOP, :] = blank
-
-    @pl.when(is_last)
-    def _():
-        u[:, TOP + points : rows, :] = blank
-
-    for i in range(2):
-        turned = jnp.transpose(out_raw[i])
-        u[i, TOP : TOP + points, :] = turned
-        acc[i] = turned
-
     def slope_of(i):
         near = u[i, TOP : TOP + 8, :]
         return (-3.0 * near[0:1] + 4.0 * near[1:2] - near[2:3]) * (0.5 / spacing)
@@ -206,12 +193,6 @@
         both = jnp.concatenate([slope_of(0), slope_of(1)], axis=0)
         sgot[k] = both.astype(BF16)
 
-    @pl.when(is_root)
-    def _():
-        stage_slope(0)
-
-    for one in loads[6:9]:
-        one.wait()
     line = lax.broadcasted_iota(jnp.int32, (rows, 1), 0)
     inside = jnp.logical_and(
         jnp.logical_or(line >= TOP, has_left), jnp.logical_or(line < TOP + points, has_right)
@@ -238,13 +219,10 @@
     def factor_of(k):
         return time_step / (k + 1) if isinstance(k, int) else time_step / (k + 1).astype(F32)
 
-    def close_grid(k):
+    def edge_of(k):
         drain(bgot2.at[k, pl.ds(0, 15)], brecv2.at[k])
         edge = jnp.sum(bgot2[k], axis=0) * (-kinetic * factor_of(k))
-        u[0, TOP : TOP + 1, :] += edge[1:2]
-        u[1, TOP : TOP + 1, :] -= edge[0:1]
-        acc[0, 0:1, :] += edge[1:2]
-        acc[1, 0:1, :] -= edge[0:1]
+        return edge[1:2], -edge[0:1]
 
     def send_boundary(k):
         @pl.when(is_plane_root)
@@ -311,9 +289,19 @@
         return lax.dot_general(masked, ampv[...], NT, preferred_element_type=F32)
 
     def next_slope(k):
-        close_grid(k)
-        stage_slope(k + 1)
+        fixes = edge_of(k)
+        slopes = [slope_of(i) - (1.5 / spacing) * fixes[i] for i in range(2)]
+        sgot[k + 1] = jnp.concatenate(slopes, axis=0).astype(BF16)
         send_slope(k + 1)
+        for i in range(2):
+            u[i, TOP : TOP + 1, :] += fixes[i]
+            acc[i, 0:1, :] += fixes[i]
+
+    def last_column(k):
+        fixes = edge_of(k)
+        columns = jnp.transpose(jnp.concatenate([*fixes, jnp.zeros((6, channels), F32)], axis=0))
+        for i in range(2):
+            outer_out[i, :, 0:1] += columns[:, i : i + 1]
 
     def finish(k, image0, image1):
         image0 = jnp.where(live0, image0, 0.0)
@@ -361,8 +349,25 @@
             stage1.at[ty * 2 + tx // 2], got1.at[plane], send1, recv1, s, dev_of(ty, zl, tx)
         ).start()
 
+    loads[5].wait()
+    blank = jnp.zeros((2, TOP, channels), F32)
+
     @pl.when(is_root)
     def _():
+        u[:, 0:TOP, :] = blank
+
+    @pl.when(is_last)
+    def _():
+        u[:, TOP + points : rows, :] = blank
+
+    for i in range(2):
+        turned = jnp.transpose(out_raw[i])
+        u[i, TOP : TOP + points, :] = turned
+        acc[i] = turned
+
+    @pl.when(is_root)
+    def _():
+        stage_slope(0)
         send_slope(0)
 
     @pl.when(has_left)
@@ -373,6 +378,8 @@
     def _():
         to_right.start()
 
+    for one in loads[6:9]:
+        one.wait()
     got1[plane] = stage1[y * 2 + x // 2]
     drain(got1.at[pl.ds(0, 15)], recv1)
 
@@ -497,7 +504,7 @@
 
         outer_update(k)
 
-        @pl.when(jnp.logical_and(k == TERMS - 1, jnp.logical_not(is_root)))
+        @pl.when(k == TERMS - 1)
         def _():
             for i in range(2):
                 outer_out[i] = jnp.transpose(acc[i])
@@ -532,6 +539,10 @@
         def _():
             next_slope(k)
 
+        @pl.when(jnp.logical_and(is_root, k == TERMS - 1))
+        def _():
+            last_column(k)
+
         @pl.when(s == 1)
         def _():
             drain(above_d.at[k], recvx.at[k])
@@ -584,12 +595,6 @@
 
     inner_out[0] = wsum[0:2]
     inner_out[1] = wsum[2:4]
-
-    @pl.when(is_root)
-    def _():
-        close_grid(TERMS - 1)
-        for i in range(2):
-            outer_out[i] = jnp.transpose(acc[i])
 
 
 def deliver(inner_v, outer_v, inner_out, outer_out, sems):

time: 50.6 us -> 50.3 us (level)
  no operation moved by 1% of the time
where the time goes in v5:
time: 50.3 us; the launch traced here: 50.2 us
  Pallas kernels  49.6 us (99%)
  between operations  0.64 us (1%)
    pallas_call x1, Pallas kernels, on_device(): pl.pallas_call(kernel, out_shape=(pltpu.VMEM(inner.shape, F32), pltpu.VME...  48.6 us

profile of v5, /device:TPU:1, one launch (start us, length us, event | category | flops | bytes accessed | tf_op | source)
XLA Modules:
  0.0 50.2 jit_solution(6381065001569498058)
XLA Ops:
  0.6 48.6 %shard_map.104 = (f32[2,2,64]{2,1,0:T(2,128)S(1)}, f32[2,800,128]{2,1,0:T(8,128)S(1)}) custom-call(s32[8]{0:T(128)} %sizes_in.1, f32[2,2,64]{2,1,0:T(2,128)} %inner.1, bf16[2,64,4096]{2,1,0:T(8,128)(2,1)} %ham.1, bf16[2,64,4096]{2,1,0:T(8,128)(2,1)} %dip.1, bf16[64,800]{1,0:T(8,128)(2,1)} %bitcast.2, s32[1,800]{1,0:T(1,128)} %bitcast.3, ...), custom_call_target="tpu_custom_call" | custom-call | tf_op jit(solution)/shard_map/pallas_call | solution.py:618
  49.3 0.9 %shard_map.105 = (f32[2,2,64]{2,1,0:T(2,128)}, f32[2,800,128]{2,1,0:T(8,128)}) custom-call(f32[2,2,64]{2,1,0:T(2,128)S(1)} %get-tuple-element.4.inner_v, f32[2,800,128]{2,1,0:T(8,128)S(1)} %get-tuple-element.5.outer_v), custom_call_target="tpu_custom_call" | custom-call | tf_op jit(solution)/shard_map/pallas_call | solution.py:672

commit v6 on v5

--- a/solution.py
+++ b/solution.py
@@ -31,6 +31,15 @@
     [(oy, ox) for oy in range(4) for ox in range(4) if (oy, ox) != (0, 0)],
     key=lambda o: -(torus(o[0]) + torus(o[1])),
 )
+
+
+def added(terms):
+    chains = [terms[n].astype(F32) for n in range(8)]
+    for n in range(8, len(terms)):
+        chains[n % 8] += terms[n].astype(F32)
+    while len(chains) > 1:
+        chains = [chains[n] + chains[n + 1] for n in range(0, len(chains), 2)]
+    return chains[0]
 
 
 def remote(src, dst, send, recv, sym, dev):
@@ -383,10 +392,7 @@
     got1[plane] = stage1[y * 2 + x // 2]
     drain(got1.at[pl.ds(0, 15)], recv1)
 
-    sums = got1[0, 1:5].astype(F32)
-    for p in range(1, 16):
-        sums += got1[p, 1:5].astype(F32)
-    sums = sums.astype(BF16)
+    sums = added([got1[p, 1:5] for p in range(16)]).astype(BF16)
     tiles = [got1[2 * q, 0] + got1[2 * q + 1, 0] for q in range(8)]
     for z_ in range(4):
         for q in range(8):
@@ -519,9 +525,7 @@
                 highs[:, q * 128 : (q + 1) * 128] = got[k, 2 * q, 0, 0:2] + got[k, 2 * q + 1, 0, 0:2]
             give_high.start()
 
-        sums = got[k, 0, 1].astype(F32)
-        for p in range(1, 64):
-            sums += got[k, p, 1].astype(F32)
+        sums = added([got[k, p, 1] for p in range(64)])
 
         @pl.when(is_low)
         def _():
@@ -552,10 +556,7 @@
         @pl.when(s == 2)
         def _():
             drain(below_d.at[k], recvx.at[k])
-            total = below_d[k, 0].astype(F32)
-            for p in range(1, 64):
-                total += below_d[k, p].astype(F32)
-            lower_h[k] = total[2:4]
+            lower_h[k] = added([below_d[k, p] for p in range(64)])[2:4]
 
         @pl.when(is_low)
         def _():

time: 50.3 us -> 50.3 us (level)
  no operation moved by 1% of the time
where the time goes in v6:
time: 50.3 us; the launch traced here: 50.2 us
  Pallas kernels  49.5 us (98%)
  between operations  0.64 us (1%)
    pallas_call x1, Pallas kernels, on_device(): pl.pallas_call(kernel, out_shape=(pltpu.VMEM(inner.shape, F32), pltpu.VME...  48.6 us

profile of v6, /device:TPU:1, one launch (start us, length us, event | category | flops | bytes accessed | tf_op | source)
XLA Modules:
  0.0 50.2 jit_solution(6978041233804664934)
XLA Ops:
  0.6 48.6 %shard_map.104 = (f32[2,2,64]{2,1,0:T(2,128)S(1)}, f32[2,800,128]{2,1,0:T(8,128)S(1)}) custom-call(s32[8]{0:T(128)} %sizes_in.1, f32[2,2,64]{2,1,0:T(2,128)} %inner.1, bf16[2,64,4096]{2,1,0:T(8,128)(2,1)} %ham.1, bf16[2,64,4096]{2,1,0:T(8,128)(2,1)} %dip.1, bf16[64,800]{1,0:T(8,128)(2,1)} %bitcast.2, s32[1,800]{1,0:T(1,128)} %bitcast.3, ...), custom_call_target="tpu_custom_call" | custom-call | tf_op jit(solution)/shard_map/pallas_call | solution.py:619
  49.3 0.9 %shard_map.105 = (f32[2,2,64]{2,1,0:T(2,128)}, f32[2,800,128]{2,1,0:T(8,128)}) custom-call(f32[2,2,64]{2,1,0:T(2,128)S(1)} %get-tuple-element.4.inner_v, f32[2,800,128]{2,1,0:T(8,128)S(1)} %get-tuple-element.5.outer_v), custom_call_target="tpu_custom_call" | custom-call | tf_op jit(solution)/shard_map/pallas_call | solution.py:673

commit v7 on v6

--- a/solution.py
+++ b/solution.py
@@ -600,8 +600,9 @@
 
 def deliver(inner_v, outer_v, inner_out, outer_out, sems):
     copies = [
-        pltpu.make_async_copy(outer_v, outer_out, sems.at[0]),
-        pltpu.make_async_copy(inner_v, inner_out, sems.at[1]),
+        pltpu.make_async_copy(outer_v.at[0], outer_out.at[0], sems.at[0]),
+        pltpu.make_async_copy(outer_v.at[1], outer_out.at[1], sems.at[1]),
+        pltpu.make_async_copy(inner_v, inner_out, sems.at[2]),
     ]
     for one in copies:
         one.start()
@@ -678,7 +679,7 @@
         ),
         in_specs=[pl.BlockSpec(memory_space=pltpu.VMEM)] * 2,
         out_specs=(anywhere, anywhere),
-        scratch_shapes=[dma((2,))],
+        scratch_shapes=[dma((3,))],
         compiler_params=pltpu.CompilerParams(vmem_limit_bytes=1024 * 1024),
     )(*results)
 

time: 50.3 us -> 50.3 us (level)
  no operation moved by 1% of the time
where the time goes in v7:
time: 50.3 us; the launch traced here: 50.2 us
  Pallas kernels  49.5 us (98%)
  between operations  0.64 us (1%)
    pallas_call x1, Pallas kernels, on_device(): pl.pallas_call(kernel, out_shape=(pltpu.VMEM(inner.shape, F32), pltpu.VME...  48.6 us

profile of v7, /device:TPU:1, one launch (start us, length us, event | category | flops | bytes accessed | tf_op | source)
XLA Modules:
  0.0 50.2 jit_solution(3746427667205430677)
XLA Ops:
  0.6 48.6 %shard_map.104 = (f32[2,2,64]{2,1,0:T(2,128)S(1)}, f32[2,800,128]{2,1,0:T(8,128)S(1)}) custom-call(s32[8]{0:T(128)} %sizes_in.1, f32[2,2,64]{2,1,0:T(2,128)} %inner.1, bf16[2,64,4096]{2,1,0:T(8,128)(2,1)} %ham.1, bf16[2,64,4096]{2,1,0:T(8,128)(2,1)} %dip.1, bf16[64,800]{1,0:T(8,128)(2,1)} %bitcast.2, s32[1,800]{1,0:T(1,128)} %bitcast.3, ...), custom_call_target="tpu_custom_call" | custom-call | tf_op jit(solution)/shard_map/pallas_call | solution.py:620
  49.3 0.9 %shard_map.105 = (f32[2,2,64]{2,1,0:T(2,128)}, f32[2,800,128]{2,1,0:T(8,128)}) custom-call(f32[2,2,64]{2,1,0:T(2,128)S(1)} %get-tuple-element.4.inner_v, f32[2,800,128]{2,1,0:T(8,128)S(1)} %get-tuple-element.5.outer_v), custom_call_target="tpu_custom_call" | custom-call | tf_op jit(solution)/shard_map/pallas_call | solution.py:674
